TPU v7x, 32 devices: a whole 2x2x4 slice. The times are simulated.
32 devices in a mesh: groups: 2 (over x), ctx: 16 (over z, y, core).
Axes of the slice: x: 2, y: 2, z: 4, core: 2. Of those that a mesh axis runs over, the one named last changes fastest.
Arguments:
- gate_short: bfloat16 [4096, 4096], P(('groups', 'ctx')), parts along dimension 0, may hold values from -6 to 6
- key_short: bfloat16 [4096, 4096], P(('groups', 'ctx')), parts along dimension 0, may hold values from -6 to 6
- value_short: bfloat16 [4096, 4096], P(('groups', 'ctx')), parts along dimension 0, may hold values from -6 to 6
- gate_long: bfloat16 [4096, 4096], P(('groups', 'ctx')), parts along dimension 0, may hold values from -6 to 6
- doc_ids: int32 [4096], P(('groups', 'ctx')), parts along dimension 0, may hold values from 0 to 7, never falling along the last dimension, each value on 1 to 512 neighbouring positions
- se_filter: float32 [7, 256], replicated, may hold values from -2 to 2
- long_filter: bfloat16 [256, 512], replicated, may hold values from -1.25 to 1.25
Outputs:
- scored: bfloat16 [4096, 4096], P(('groups', 'ctx')), parts along dimension 0
There are 2 independent parts, one for each index of `groups`. A program takes and returns all parts, laid end to end along the dimension named above; an argument that names none is the same for every part. Nothing has to cross between parts.
Inputs may be any that keep to these rules, and one draw needn't show every extreme that they name: doc_ids never falls along the rows of a group; each document holds 1 to 512 consecutive rows, and one holds exactly 512.
All inputs are finite; a program needn't handle non-finite values.
Results may differ from a plain program's by a relative error of at most 0.0057.
Values may be sent and summed in bfloat16 or wider, within the bound.
A program may use at most 192 MiB of HBM per device.

v0:
```python
import functools

import jax
import jax.numpy as jnp
from jax import lax
from jax.experimental import pallas as pl
from jax.experimental.pallas import tpu as pltpu
from jax.sharding import PartitionSpec as P

MAXDOC = 512
REACH = 4
RIM = 16
STEP = 16
LAG = 1
LANES = 128
CHUNKS = 8
MESH = pl.DeviceIdType.MESH


def kernel(
    count, gs_ref, k_ref, v_ref, gl_ref, doc_ref, se_ref, h_ref, out_ref,
    own, own_doc, rim_out, rim_in, got, got_doc, taps, rev, near_w, acc, agree, far_mask, near_mask,
    send_sem, recv_sem, doc_send, doc_recv, rim_send, rim_recv,
):
    rows, chans = gs_ref.shape
    tap_count = se_ref.shape[0]
    filters = h_ref.shape[0]
    width = chans // CHUNKS
    tiles = width // LANES
    fgroup = chans // filters
    per_tile = LANES // fgroup
    half = rows // 2
    span = MAXDOC + rows
    f32, bf16 = jnp.float32, jnp.bfloat16

    me = lax.axis_index("ctx")
    at = lax.rem(me, REACH)
    core = lax.rem(me, 2)
    upper = at // 2
    core_mate = me + 1 - 2 * core
    row_mate = me + 2 - 4 * upper
    has_prev = me >= REACH
    has_next = me + REACH < count
    is_first = me == 0
    is_last = me == count - 1

    barrier = pltpu.get_barrier_semaphore()

    def greet(target):
        pl.semaphore_signal(barrier, inc=1, device_id={"ctx": target}, device_id_type=MESH)

    greet(core_mate)
    greet(row_mate)
    pl.when(has_prev)(lambda: greet(me - REACH))
    pl.when(has_next)(lambda: greet(me + REACH))
    pl.when(me > 0)(lambda: greet(me - 1))
    pl.when(me < count - 1)(lambda: greet(me + 1))

    doc_row = jnp.broadcast_to(doc_ref[...].astype(f32), (rows, rows))
    doc_col = doc_row.T
    near_mask[...] = (doc_row == doc_col).astype(bf16)
    own_doc[...] = doc_col.astype(bf16)
    kv_tail = k_ref[rows - RIM :, :].astype(f32) * v_ref[rows - RIM :, :].astype(f32)
    rim_out[:, :chans] = kv_tail.astype(bf16)
    rim_out[:, chans:] = doc_col[rows - RIM :, :].astype(bf16)

    peers = 2 + has_prev.astype(jnp.int32) + has_next.astype(jnp.int32)
    peers = peers + (me > 0).astype(jnp.int32) + (me < count - 1).astype(jnp.int32)
    pl.semaphore_wait(barrier, peers)

    def remote(src, dst, ssem, rsem, target):
        return pltpu.make_async_remote_copy(
            src_ref=src, dst_ref=dst, send_sem=ssem, recv_sem=rsem,
            device_id={"ctx": target}, device_id_type=MESH,
        )

    def rim_copy(target):
        return remote(rim_out, rim_in, rim_send, rim_recv, target)

    pl.when(me < count - 1)(lambda: rim_copy(me + 1).start())

    def block_copy(slot, j, src, target):
        return remote(src, got.at[slot, j], send_sem.at[slot, j], recv_sem.at[slot, j], target)

    def doc_copy(slot, src, target):
        return remote(src, got_doc.at[slot], doc_send.at[slot], doc_recv.at[slot], target)

    def start(slot, j, source, target):
        block, docs = (own.at[j], own_doc) if source is None else (got.at[source, j], got_doc.at[source])
        pl.when(j == 0)(lambda: doc_copy(slot, docs, target).start())
        block_copy(slot, j, block, target).start()

    def await_recv(slot, j):
        pl.when(j == 0)(lambda: doc_copy(slot, own_doc, core_mate).wait_recv())
        block_copy(slot, j, own.at[j], core_mate).wait_recv()

    def await_send(slot, j):
        pl.when(j == 0)(lambda: doc_copy(slot, own_doc, core_mate).wait_send())
        block_copy(slot, j, own.at[j], core_mate).wait_send()

    @pl.when(is_first)
    def _():
        rim_in[:, :chans] = jnp.zeros((RIM, chans), bf16)
        rim_in[:, chans:] = jnp.full((RIM, LANES), -1.0, bf16)

    @pl.when(me > 0)
    def _():
        rim_copy(core_mate).wait_recv()

    doc_ext = jnp.concatenate([rim_in[:, chans:].astype(f32), doc_col], 0)
    for tap in range(tap_count):
        agree[tap] = (doc_ext[RIM - tap : RIM - tap + rows] == doc_col).astype(f32)

    left_over, terms = se_ref[...], []
    for _ in range(3):
        term = left_over.astype(bf16).astype(f32)
        left_over = left_over - term
        terms += [term, jnp.zeros((8 - tap_count, filters), f32)]
    se_parts = jnp.concatenate(terms, 0).astype(bf16)

    def short_chunk(j, _):
        source = lax.broadcasted_iota(jnp.int32, (filters, width), 0)
        target = lax.broadcasted_iota(jnp.int32, (filters, width), 1) // fgroup
        spread = jnp.where(source - j * (width // fgroup) == target, 1.0, 0.0).astype(bf16)
        parts = jnp.dot(se_parts, spread, preferred_element_type=f32)
        widened = parts[0:tap_count] + parts[8 : 8 + tap_count] + parts[16 : 16 + tap_count]
        for tile in range(tiles):
            lanes = pl.ds(pl.multiple_of(j * width + tile * LANES, LANES), LANES)
            kv = (k_ref[:, lanes].astype(f32) * v_ref[:, lanes].astype(f32)).astype(bf16).astype(f32)
            ext = jnp.concatenate([rim_in[:, lanes].astype(f32), kv], 0)
            weights = widened[:, tile * LANES : (tile + 1) * LANES]
            total = kv * weights[0:1, :]
            for tap in range(1, tap_count):
                shifted = ext[RIM - tap : RIM - tap + rows]
                total = total + (shifted * agree[tap]) * weights[tap : tap + 1, :]
            mixed = gs_ref[:, lanes].astype(f32) * total
            own[j, :, tile * LANES : (tile + 1) * LANES] = mixed.astype(bf16)
        pl.when(has_next)(lambda: start(0, j, None, me + REACH))
        pl.when(upper == 0)(lambda: start(2, j, None, row_mate))
        pl.when(core == 0)(lambda: start(1, j, None, core_mate))
        return 0

    lax.fori_loop(0, CHUNKS, short_chunk, 0)

    @pl.when(jnp.logical_not(has_prev))
    def _():
        got[0] = jnp.zeros(got.shape[1:], bf16)
        got_doc[0] = jnp.full(got_doc.shape[1:], -1.0, bf16)

    for piece in range(span // LANES):
        lag = lax.broadcasted_iota(jnp.int32, (MAXDOC, LANES), 0)
        pos = lax.broadcasted_iota(jnp.int32, (MAXDOC, LANES), 1) + piece * LANES
        flip = jnp.where(lag + pos == MAXDOC, 1.0, 0.0).astype(bf16)
        rev[:, piece * LANES : (piece + 1) * LANES] = jnp.dot(
            h_ref[...], flip, preferred_element_type=f32
        )

    lane_group = lax.broadcasted_iota(jnp.int32, (1, LANES), 1) // fgroup

    def pick(result, height, lanes):
        picked = result[0:height, lanes]
        for g in range(1, per_tile):
            picked = jnp.where(lane_group == g, result[g * height : (g + 1) * height, lanes], picked)
        return picked

    def prepare(j, tile):
        ct = j * tiles + tile
        first = pl.multiple_of(ct * per_tile, per_tile)
        filt = rev[pl.ds(first, per_tile), :]
        for g in range(per_tile):
            line = jnp.broadcast_to(filt[g : g + 1, :], (STEP, span))
            base = pltpu.roll(line, 0, 1, stride=1, stride_axis=0).astype(bf16)
            tail = base[:, span - 2 * LANES :]
            for r in range(rows // STEP):
                low = slice(r * STEP, (r + 1) * STEP)
                if r * STEP < half:
                    turned = base if r == 0 else pltpu.roll(base, r * STEP, 1)
                    at_row = pl.multiple_of((ct * per_tile + g) * half + r * STEP, STEP)
                    taps[pl.ds(at_row, STEP), :] = turned[:, :MAXDOC]
                    near = turned[:, MAXDOC:]
                else:
                    near = pltpu.roll(tail, r * STEP, 1)[:, LANES:]
                near_w[g * rows + r * STEP : g * rows + (r + 1) * STEP, :] = near * near_mask[low, :]
        block = own[j, :, pl.ds(pl.multiple_of(tile * LANES, LANES), LANES)]
        result = jnp.dot(near_w[...], block, preferred_element_type=f32)
        acc[ct] = pick(result, rows, slice(0, LANES))

    leader = jnp.broadcast_to(doc_row[0:1, 0:1], (rows, LANES))
    near_mask_out = (doc_col == leader).astype(f32)
    agree[0] = near_mask_out

    def far(j, tile):
        ct = j * tiles + tile
        lanes = slice(tile * LANES, (tile + 1) * LANES)
        pieces = []
        for w in range(REACH):
            q = lax.rem(at + w, REACH)
            slot = (q // 2 + at // 2) % 2 * 2 + (q + at) % 2
            pieces.append(got[slot, j, :, lanes] * far_mask[w])
        left = jnp.concatenate(pieces, 0)
        right = jnp.concatenate([left[half:], jnp.zeros((half, LANES), bf16)], 0)
        base = pl.multiple_of(ct * per_tile * half, per_tile * half)
        result = jnp.dot(
            taps[pl.ds(base, per_tile * half), :],
            jnp.concatenate([left, right], 1),
            preferred_element_type=f32,
        )
        both = jnp.concatenate(
            [pick(result, half, slice(0, LANES)), pick(result, half, slice(LANES, 2 * LANES))], 0
        )
        total = acc[ct] + both * agree[0]
        wide = pl.ds(pl.multiple_of(ct * LANES, LANES), LANES)
        out_ref[:, wide] = (gl_ref[:, wide].astype(f32) * total).astype(bf16)

    def step(s, _):
        @pl.when(s < CHUNKS)
        def _():
            lax.fori_loop(0, tiles, lambda tile, c: (prepare(s, tile), c)[1], 0)
            pl.when(has_prev)(lambda: await_recv(0, s))
            pl.when(upper == 1)(lambda: start(2, s, 0, row_mate))
            pl.when(core == 1)(lambda: start(1, s, 0, core_mate))

        @pl.when((s >= LAG) & (s < CHUNKS + LAG))
        def _():
            await_recv(2, s - LAG)
            start(3, s - LAG, 2, core_mate)

        @pl.when(s >= 2 * LAG)
        def _():
            j = s - 2 * LAG
            await_recv(1, j)
            await_recv(3, j)

            @pl.when(j == 0)
            def _():
                for w in range(REACH):
                    q = lax.rem(at + w, REACH)
                    slot = (q // 2 + at // 2) % 2 * 2 + (q + at) % 2
                    far_mask[w] = (got_doc[slot].astype(f32) == leader).astype(bf16)

            for tile in range(tiles):
                far(j, tile)

        return 0

    lax.fori_loop(0, CHUNKS + 2 * LAG, step, 0)

    def drain(j, _):
        pl.when(has_next)(lambda: await_send(0, j))
        for slot in (1, 2, 3):
            await_send(slot, j)
        return 0

    lax.fori_loop(0, CHUNKS, drain, 0)
    pl.when(me < count - 1)(lambda: rim_copy(core_mate).wait_send())


def body(gate_short, key_short, value_short, gate_long, doc_ids, se_filter, long_filter):
    rows, chans = gate_short.shape
    tap_count, filters = se_filter.shape
    fgroup = chans // filters
    count = lax.axis_size("ctx")
    assert rows * REACH == MAXDOC and rows == LANES and count % REACH == 0
    width = chans // CHUNKS
    bf16, f32 = jnp.bfloat16, jnp.float32
    vmem = pl.BlockSpec(memory_space=pltpu.VMEM)
    return pl.pallas_call(
        functools.partial(kernel, count),
        out_shape=jax.ShapeDtypeStruct((rows, chans), bf16),
        in_specs=[vmem] * 7,
        out_specs=vmem,
        scratch_shapes=[
            pltpu.VMEM((CHUNKS, rows, width), bf16),
            pltpu.VMEM((rows, LANES), bf16),
            pltpu.VMEM((RIM, chans + LANES), bf16),
            pltpu.VMEM((RIM, chans + LANES), bf16),
            pltpu.VMEM((REACH, CHUNKS, rows, width), bf16),
            pltpu.VMEM((REACH, rows, LANES), bf16),
            pltpu.VMEM((filters * rows // 2, MAXDOC), bf16),
            pltpu.VMEM((filters, MAXDOC + rows), f32),
            pltpu.VMEM((LANES // fgroup * rows, rows), bf16),
            pltpu.VMEM((chans // LANES, rows, LANES), f32),
            pltpu.VMEM((tap_count, rows, LANES), f32),
            pltpu.VMEM((REACH, rows, LANES), bf16),
            pltpu.VMEM((rows, rows), bf16),
            pltpu.SemaphoreType.DMA((REACH, CHUNKS)),
            pltpu.SemaphoreType.DMA((REACH, CHUNKS)),
            pltpu.SemaphoreType.DMA((REACH,)),
            pltpu.SemaphoreType.DMA((REACH,)),
            pltpu.SemaphoreType.DMA,
            pltpu.SemaphoreType.DMA,
        ],
        compiler_params=pltpu.CompilerParams(
            collective_id=0, has_side_effects=True, vmem_limit_bytes=56 * 1024 * 1024
        ),
    )(gate_short, key_short, value_short, gate_long, doc_ids.reshape(1, rows), se_filter, long_filter)


def solution(mesh):
    placed = P(("groups", "ctx"), None)
    return jax.shard_map(
        body,
        mesh=mesh,
        in_specs=(placed, placed, placed, placed, P(("groups", "ctx")), P(), P()),
        out_specs=placed,
        check_vma=False,
    )
```

profile of v0, /device:TPU:0, one launch (start us, length us, event | category | flops | bytes accessed | tf_op | source)
XLA Modules:
  0.0 46.2 jit_solution(5442845827704111965)
XLA Ops:
  0.0 43.9 %shard_map.73 = bf16[128,4096]{1,0:T(8,128)(2,1)} custom-call(bf16[128,4096]{1,0:T(8,128)(2,1)} %gs_ref.1, bf16[128,4096]{1,0:T(8,128)(2,1)} %k_ref.1, bf16[128,4096]{1,0:T(8,128)(2,1)} %v_ref.1, bf16[128,4096]{1,0:T(8,128)(2,1)} %gl_ref.1, s32[1,128]{1,0:T(1,128)} %bitcast.1, f32[7,256]{1,0:T(8,128)} %se_ref.1, bf16[256,512]{1,0:T(8,128)(2,1)} %h_ref.1), custom_call_target="tpu_custom_call" | custom-call | tf_op jit(solution)/shard_map/pallas_call | solution.py:267
  43.9 2.3 %copy.9 = bf16[128,4096]{1,0:T(8,128)(2,1)} copy(bf16[128,4096]{1,0:T(8,128)(2,1)} %shard_map.73) | data formatting | bytes 2097152
where the time goes:
time: 46.3 us; the launch traced here: 46.2 us
  Pallas kernels  43.9 us (95%)
  local copies, waits for them, and re-layouts  2.29 us (5%)
    pallas_call x1, Pallas kernels, body(): pl.pallas_call(functools.partial(kernel, count), out_shape=jax.ShapeDtype...  43.9 us
    unnamed x1, local copies, waits for them, and re-layouts  2.29 us

commit v1 on v0

v1 whole, which is shorter than its diff:
```python
import functools

import jax
import jax.numpy as jnp
from jax import lax
from jax.experimental import pallas as pl
from jax.experimental.pallas import tpu as pltpu
from jax.sharding import PartitionSpec as P

MAXDOC = 512
REACH = 4
RIM = 8
LANES = 128
PACK = 16
MSGS = 16
EARLY = 2
LAG1 = 2
LAG2 = 5
BASE = 32
MESH = pl.DeviceIdType.MESH


def kernel(
    count, gs_hbm, k_hbm, v_hbm, gl_hbm, doc_hbm, se_hbm, h_hbm, out_ref,
    gs_ref, k_ref, v_ref, gl_ref, doc_ref, se_ref, h_ref, tail_k, tail_v,
    own, got, doc_out, got_doc, rim_out, rim_in, se_two, doc_ext, ext, agree,
    rev, taps, acc, near_mask, far_mask, out_mask,
    in_sem, one_sem, send_sem, recv_sem, head_send, head_recv, doc_send, doc_recv, rim_send, rim_recv,
):
    rows, chans = gs_ref.shape
    tap_count, filters = se_ref.shape
    fgroup = chans // filters
    per_tile = LANES // fgroup
    tiles = chans // LANES
    each = tiles // MSGS
    width = each * LANES
    half = rows // 2
    body_rows = rows - RIM
    f32, bf16, i32 = jnp.float32, jnp.bfloat16, jnp.int32

    me = lax.axis_index("ctx")
    at = lax.rem(me, REACH)
    core = lax.rem(me, 2)
    upper = at // 2
    core_mate = me + 1 - 2 * core
    row_mate = me + 2 - 4 * upper
    has_prev = me >= REACH
    has_next = me + REACH < count

    def local(src, dst, sem):
        return pltpu.make_async_copy(src, dst, sem)

    def piece(i, j):
        src, dst = ((k_hbm, k_ref), (v_hbm, v_ref), (gs_hbm, gs_ref))[i]
        cols = pl.ds(pl.multiple_of(j * width, width), width)
        return local(src.at[:, cols], dst.at[:, cols], in_sem.at[i, j])

    doc_in = local(doc_hbm, doc_ref, one_sem.at[0])
    tails = [
        local(k_hbm.at[pl.ds(rows - RIM, RIM), :], tail_k, one_sem.at[1]),
        local(v_hbm.at[pl.ds(rows - RIM, RIM), :], tail_v, one_sem.at[2]),
    ]
    se_in = local(se_hbm, se_ref, one_sem.at[3])
    h_in = local(h_hbm, h_ref, one_sem.at[4])
    gl_in = local(gl_hbm, gl_ref, one_sem.at[5])

    doc_in.start()
    tails[0].start()
    tails[1].start()
    se_in.start()
    for i in range(3):
        piece(i, 0).start()

    barrier = pltpu.get_barrier_semaphore()

    def greet(target):
        pl.semaphore_signal(barrier, inc=1, device_id={"ctx": target}, device_id_type=MESH)

    peers = jnp.int32(0)
    for d in range(1, REACH + 1):
        pl.when(me >= d)(lambda d=d: greet(me - d))
        pl.when(me + d < count)(lambda d=d: greet(me + d))
        peers = peers + (me >= d).astype(i32) + (me + d < count).astype(i32)

    def fetch(j, _):
        for i in range(3):
            piece(i, j).start()
        return 0

    lax.fori_loop(1, MSGS, fetch, 0)
    h_in.start()
    gl_in.start()

    lane = lax.broadcasted_iota(i32, (rows, LANES), 1)
    row = lax.broadcasted_iota(i32, (rows, LANES), 0)

    doc_in.wait()
    doc_row = jnp.broadcast_to(doc_ref[...].astype(f32), (rows, LANES))
    doc_col = doc_row.T
    doc_out[...] = doc_row[0:8]
    doc_ext[RIM:, :] = doc_col
    tails[0].wait()
    tails[1].wait()
    rim_out[...] = (tail_k[...].astype(f32) * tail_v[...].astype(f32)).astype(bf16)

    pl.semaphore_wait(barrier, peers)

    def remote(src, dst, ssem, rsem, target):
        return pltpu.make_async_remote_copy(
            src_ref=src, dst_ref=dst, send_sem=ssem, recv_sem=rsem,
            device_id={"ctx": target}, device_id_type=MESH,
        )

    def rim_copy(target):
        return remote(rim_out, rim_in, rim_send, rim_recv, target)

    def doc_copy(d, target):
        slot = REACH - d
        return remote(doc_out, got_doc.at[slot], doc_send.at[slot], doc_recv.at[slot], target)

    pl.when(me + 1 < count)(lambda: rim_copy(me + 1).start())
    for d in range(1, REACH + 1):
        pl.when(me + d < count)(lambda d=d: doc_copy(d, me + d).start())

    def msg_copy(slot, m, source, target):
        block = own if source is None else got.at[source]
        part = (pl.ds(m * each, each), pl.ds(RIM, body_rows))
        return remote(block.at[part], got.at[(slot, *part)], send_sem.at[slot, m], recv_sem.at[slot, m], target)

    def head_copy(slot, source, target):
        block = own if source is None else got.at[source]
        part = (pl.ds(0, tiles), pl.ds(0, RIM))
        return remote(block.at[part], got.at[(slot, *part)], head_send.at[slot], head_recv.at[slot], target)

    def send_own(copy):
        pl.when(has_next)(lambda: copy(0, None, me + REACH).start())
        pl.when(upper == 0)(lambda: copy(2, None, row_mate).start())
        pl.when(core == 0)(lambda: copy(1, None, core_mate).start())

    def msg(m):
        return lambda slot, source, target: msg_copy(slot, m, source, target)

    for tap in range(1, tap_count):
        agree[tap, RIM:, :] = (doc_ext[2 * RIM - tap : RIM + rows - tap, :] == doc_col[RIM:]).astype(f32)

    se_in.wait()
    for part in range(filters // LANES):
        se_two[part, 0:tap_count, :] = se_ref[:, part * LANES : (part + 1) * LANES]
        se_two[part, tap_count:, :] = jnp.zeros((8 - tap_count, LANES), f32)

    tiles_per_part = LANES // per_tile
    spread = lax.broadcasted_iota(i32, (8, LANES), 1) // fgroup

    def weights_of(ct):
        index = spread + lax.rem(ct, tiles_per_part) * per_tile
        return jnp.take_along_axis(se_two[ct // tiles_per_part], index, axis=1)

    def lanes_of(ct):
        return pl.ds(pl.multiple_of(ct * LANES, LANES), LANES)

    def product(ct, part):
        lanes = lanes_of(ct)
        return (k_ref[part, lanes].astype(f32) * v_ref[part, lanes].astype(f32)).astype(bf16).astype(f32)

    def short_body(j, _):
        for i in range(3):
            piece(i, j).wait()
        for u in range(each):
            ct = j * each + u
            weights = weights_of(ct)
            kv = product(ct, slice(None))
            ext[u, RIM:, :] = kv
            total = kv[RIM:] * weights[0:1, :]
            for tap in range(1, tap_count):
                shifted = ext[u, 2 * RIM - tap : RIM + rows - tap, :]
                total = total + (shifted * agree[tap, RIM:, :]) * weights[tap : tap + 1, :]
            mixed = gs_ref[RIM:, lanes_of(ct)].astype(f32) * total
            own[ct, RIM:, :] = mixed.astype(bf16)
        pl.when(j < EARLY)(lambda: send_own(msg(j)))
        return 0

    lax.fori_loop(0, MSGS, short_body, 0)

    h_in.wait()
    lag = lax.broadcasted_iota(i32, (LANES, LANES), 0)
    pos = lax.broadcasted_iota(i32, (LANES, LANES), 1)
    flip = jnp.where(lag == lax.rem(LANES - pos, LANES), 1.0, 0.0).astype(bf16)
    for d in range(REACH):
        cols = slice(d * LANES, (d + 1) * LANES)
        rev[:, cols] = jnp.dot(h_ref[:, cols], flip, preferred_element_type=f32)

    low = lane[:half] < half
    causal = lane[:half] <= row[:half]
    same_low = doc_col[:half] == doc_row[:half]
    same_high = doc_col[half:] == pltpu.roll(doc_row[:half], half, 1)
    late = same_high.astype(f32)
    early = causal.astype(f32) * same_low.astype(f32)
    near_mask[0] = jnp.where(low, early, late).astype(bf16)
    near_mask[1] = jnp.where(low, causal.astype(f32) * late, 0.0).astype(bf16)
    leader = jnp.broadcast_to(doc_row[0:1, 0:1], (rows, LANES))
    out_mask[...] = (doc_col == leader).astype(f32)

    for w in range(REACH):
        pl.when(me >= REACH - w)(lambda w=w: doc_copy(REACH - w, core_mate).wait_recv())

        @pl.when(me < REACH - w)
        def _():
            got_doc[w] = jnp.full((8, LANES), -1.0, f32)

        source_col = jnp.broadcast_to(got_doc[w, 0:1, :], (rows, LANES)).T
        far_mask[w] = (source_col == leader).astype(bf16)
        if w == REACH - 1:
            doc_ext[0:RIM, :] = source_col[rows - RIM :]

    @pl.when(me == 0)
    def _():
        rim_in[...] = jnp.zeros((RIM, chans), bf16)

    @pl.when(me > 0)
    def _():
        rim_copy(core_mate).wait_recv()

    for tap in range(1, tap_count):
        agree[tap, 0:RIM, :] = (doc_ext[RIM - tap : 2 * RIM - tap, :] == doc_col[0:RIM]).astype(f32)

    def short_head(j, _):
        for u in range(4):
            ct = j * 4 + u
            weights = weights_of(ct)
            kv = product(ct, slice(0, RIM))
            ext[u, 0:RIM, :] = rim_in[:, lanes_of(ct)].astype(f32)
            ext[u, RIM : 2 * RIM, :] = kv
            total = kv * weights[0:1, :]
            for tap in range(1, tap_count):
                shifted = ext[u, RIM - tap : 2 * RIM - tap, :]
                total = total + (shifted * agree[tap, 0:RIM, :]) * weights[tap : tap + 1, :]
            mixed = gs_ref[0:RIM, lanes_of(ct)].astype(f32) * total
            own[ct, 0:RIM, :] = mixed.astype(bf16)
        return 0

    lax.fori_loop(0, tiles // 4, short_head, 0)
    send_own(head_copy)

    def send_rest(j, _):
        send_own(msg(j))
        return 0

    lax.fori_loop(EARLY, MSGS, send_rest, 0)

    @pl.when(jnp.logical_not(has_prev))
    def _():
        got[0] = jnp.zeros(got.shape[1:], bf16)

    gl_in.wait()

    tile_group = lax.broadcasted_iota(i32, (1, LANES), 1) // fgroup
    half_group = lax.rem(tile_group, per_tile // 2)
    low_half = lax.broadcasted_iota(i32, (1, LANES), 1) < half

    def pick(result, group, groups, height, lanes):
        picked = result[0:height, lanes]
        for g in range(1, groups):
            picked = jnp.where(group == g, result[g * height : (g + 1) * height, lanes], picked)
        return picked

    below = [lane[0:PACK] <= row[0:PACK] + r * PACK for r in range(BASE // PACK)]

    def prepare(ct):
        first = pl.multiple_of(ct * per_tile, per_tile)
        filt = rev[pl.ds(first, per_tile), :]
        zero = jnp.zeros((PACK, LANES), bf16)
        near = []
        for g in range(per_tile):
            ring = []
            for d in range(REACH):
                line = jnp.broadcast_to(filt[g : g + 1, d * LANES : (d + 1) * LANES], (PACK, LANES))
                ring.append(pltpu.roll(line, 0, 1, stride=1, stride_axis=0).astype(bf16))
            for r in range(BASE // PACK):
                turned = ring if r == 0 else [pltpu.roll(c, r * PACK, 1) for c in ring]
                at_row = g * BASE + r * PACK
                for w in range(REACH):
                    d = REACH - w
                    recent = turned[d] if d < REACH else zero
                    taps[ct, w, at_row : at_row + PACK, :] = jnp.where(below[r], recent, turned[d - 1])
            for r in range(half // PACK):
                turned = ring[0] if r == 0 else pltpu.roll(ring[0], r * PACK, 1)
                at_mask = slice(r * PACK, (r + 1) * PACK)
                near.append(jnp.concatenate([turned * near_mask[0, at_mask], turned * near_mask[1, at_mask]], 1))
        block = own[ct]
        first_half, second_half = block[:half], block[half:]
        none = jnp.zeros((half, LANES), bf16)
        right = jnp.concatenate(
            [
                jnp.concatenate([first_half, none, none, none], 0),
                jnp.concatenate([none, first_half, second_half, none], 0),
            ],
            1,
        )
        result = jnp.dot(jnp.concatenate(near, 0), right, preferred_element_type=f32)
        acc[ct, 0:half, :] = pick(result, tile_group, per_tile, half, slice(0, LANES))
        acc[ct, half:, :] = pick(result, tile_group, per_tile, half, slice(LANES, 2 * LANES))

    slots = []
    for w in range(REACH):
        q = lax.rem(at + w, REACH)
        slots.append(lax.rem(q // 2 + upper, 2) * 2 + lax.rem(q + at, 2))

    def far(ct):
        left = jnp.concatenate([got[slots[w], ct] * far_mask[w] for w in range(REACH)], 0)
        gap = jnp.zeros((BASE, LANES), bf16)
        later = jnp.concatenate([left[BASE:], gap], 0)
        outs = []
        for h in range(2):
            if h == 0:
                pair = jnp.where(low_half, left, pltpu.roll(later, half, 1))
            else:
                pair = jnp.where(low_half, pltpu.roll(left, half, 1), later)
            wide = jnp.concatenate([pair, jnp.concatenate([pair[2 * BASE :], gap, gap], 0)], 1)
            height = per_tile // 2 * BASE
            lhs = jnp.concatenate([taps[ct, w, h * height : (h + 1) * height, :] for w in range(REACH)], 1)
            result = jnp.dot(lhs, wide, preferred_element_type=f32)
            outs.append(
                [pick(result, half_group, per_tile // 2, BASE, slice(p * LANES, (p + 1) * LANES)) for p in range(2)]
            )
        both = []
        for p in range(2):
            both.append(jnp.where(low_half, outs[0][p], pltpu.roll(outs[1][p], half, 1)))
            both.append(jnp.where(low_half, pltpu.roll(outs[0][p], half, 1), outs[1][p]))
        total = acc[ct] + jnp.concatenate(both, 0) * out_mask[...]
        out_ref[:, lanes_of(ct)] = (gl_ref[:, lanes_of(ct)].astype(f32) * total).astype(bf16)

    def step(s, _):
        @pl.when(s < MSGS)
        def _():
            for u in range(each):
                prepare(s * each + u)

            def relay(copy):
                pl.when(has_prev)(lambda: copy(0, None, core_mate).wait_recv())
                pl.when(upper == 1)(lambda: copy(2, 0, row_mate).start())
                pl.when(core == 1)(lambda: copy(1, 0, core_mate).start())

            pl.when(s == EARLY)(lambda: relay(head_copy))
            relay(msg(s))

        @pl.when((s >= LAG1) & (s < MSGS + LAG1))
        def _():
            def relay(copy):
                copy(2, None, core_mate).wait_recv()
                copy(3, 2, core_mate).start()

            pl.when(s == EARLY + LAG1)(lambda: relay(head_copy))
            relay(msg(s - LAG1))

        @pl.when(s >= LAG2)
        def _():
            def arrive(copy):
                copy(1, None, core_mate).wait_recv()
                copy(3, None, core_mate).wait_recv()

            pl.when(s == LAG2)(lambda: arrive(head_copy))
            arrive(msg(s - LAG2))
            for u in range(each):
                far((s - LAG2) * each + u)

        return 0

    lax.fori_loop(0, MSGS + LAG2, step, 0)

    def drain_all(copy):
        pl.when(has_next)(lambda: copy(0, None, core_mate).wait_send())
        for slot in (1, 2, 3):
            copy(slot, None, core_mate).wait_send()

    def drain(j, _):
        drain_all(msg(j))
        return 0

    lax.fori_loop(0, MSGS, drain, 0)
    drain_all(head_copy)
    pl.when(me + 1 < count)(lambda: rim_copy(core_mate).wait_send())
    for d in range(1, REACH + 1):
        pl.when(me + d < count)(lambda d=d: doc_copy(d, core_mate).wait_send())


def body(gate_short, key_short, value_short, gate_long, doc_ids, se_filter, long_filter):
    rows, chans = gate_short.shape
    tap_count, filters = se_filter.shape
    fgroup = chans // filters
    count = lax.axis_size("ctx")
    tiles = chans // LANES
    assert rows * REACH == MAXDOC and rows == LANES and count % REACH == 0
    assert tap_count <= RIM and LANES % fgroup == 0 and filters % LANES == 0
    assert tiles % MSGS == 0 and tiles % 4 == 0 and long_filter.shape[1] == MAXDOC
    bf16, f32 = jnp.bfloat16, jnp.float32
    anywhere = pl.BlockSpec(memory_space=pl.ANY)
    dma = pltpu.SemaphoreType.DMA
    return pl.pallas_call(
        functools.partial(kernel, count),
        out_shape=jax.ShapeDtypeStruct((rows, chans), bf16),
        in_specs=[anywhere] * 7,
        out_specs=pl.BlockSpec(memory_space=pltpu.VMEM),
        scratch_shapes=[
            pltpu.VMEM((rows, chans), bf16),
            pltpu.VMEM((rows, chans), bf16),
            pltpu.VMEM((rows, chans), bf16),
            pltpu.VMEM((rows, chans), bf16),
            pltpu.VMEM((1, rows), jnp.int32),
            pltpu.VMEM((tap_count, filters), f32),
            pltpu.VMEM((filters, MAXDOC), bf16),
            pltpu.VMEM((RIM, chans), bf16),
            pltpu.VMEM((RIM, chans), bf16),
            pltpu.VMEM((tiles, rows, LANES), bf16),
            pltpu.VMEM((REACH, tiles, rows, LANES), bf16),
            pltpu.VMEM((8, LANES), f32),
            pltpu.VMEM((REACH, 8, LANES), f32),
            pltpu.VMEM((RIM, chans), bf16),
            pltpu.VMEM((RIM, chans), bf16),
            pltpu.VMEM((filters // LANES, 8, LANES), f32),
            pltpu.VMEM((RIM + rows, LANES), f32),
            pltpu.VMEM((max(4, tiles // MSGS), RIM + rows, LANES), f32),
            pltpu.VMEM((tap_count, rows, LANES), f32),
            pltpu.VMEM((filters, MAXDOC), f32),
            pltpu.VMEM((tiles, REACH, LANES // fgroup * BASE, LANES), bf16),
            pltpu.VMEM((tiles, rows, LANES), f32),
            pltpu.VMEM((2, rows // 2, LANES), bf16),
            pltpu.VMEM((REACH, rows, LANES), bf16),
            pltpu.VMEM((rows, LANES), f32),
            dma((3, MSGS)),
            dma((6,)),
            dma((REACH, MSGS)),
            dma((REACH, MSGS)),
            dma((REACH,)),
            dma((REACH,)),
            dma((REACH,)),
            dma((REACH,)),
            dma,
            dma,
        ],
        compiler_params=pltpu.CompilerParams(
            collective_id=0, has_side_effects=True, vmem_limit_bytes=40 * 1024 * 1024
        ),
    )(gate_short, key_short, value_short, gate_long, doc_ids.reshape(1, rows), se_filter, long_filter)


def solution(mesh):
    placed = P(("groups", "ctx"), None)
    return jax.shard_map(
        body,
        mesh=mesh,
        in_specs=(placed, placed, placed, placed, P(("groups", "ctx")), P(), P()),
        out_specs=placed,
        check_vma=False,
    )
```

time: 46.3 us -> 48.2 us (1.041)
  local copies, waits for them, and re-layouts: 2.29 us -> 8.17 us
  Pallas kernels: 43.9 us -> 39.7 us
    unnamed x1 -> x15, local copies, waits for them, and re-layouts: 2.29 us -> 8.17 us
    pallas_call x1, Pallas kernels: 43.9 us -> 39.7 us  [body(): pl.pallas_call(functools.partial(kernel, count), out_shape=jax.ShapeDtype...]
where the time goes in v1:
time: 48.2 us; the launch traced here: 47.9 us
  Pallas kernels  39.7 us (82%)
  local copies, waits for them, and re-layouts  8.17 us (17%)
    pallas_call x1, Pallas kernels, body(): pl.pallas_call(functools.partial(kernel, count), out_shape=jax.ShapeDtype...  39.7 us
    unnamed x15, local copies, waits for them, and re-layouts  8.17 us

profile of v1, /device:TPU:0, one launch (start us, length us, event | category | flops | bytes accessed | tf_op | source)
XLA Modules:
  0.0 47.9 jit_solution(1793199198878537249)
XLA Ops:
  0.0 0.0 copy-start.6
  0.0 0.7 %copy-done.6 = s32[128]{0:T(128)S(1)} copy-done((s32[128]{0:T(128)S(1)}, s32[128]{0:T(128)}, u32[]{:S(2)}) %copy-start.6) | copy-done | bytes 536
  0.7 0.0 copy-start
  0.7 1.2 %copy-done = bf16[128,4096]{1,0:T(8,128)(2,1)S(1)} copy-done((bf16[128,4096]{1,0:T(8,128)(2,1)S(1)}, bf16[128,4096]{1,0:T(8,128)(2,1)}, u32[]{:S(2)}) %copy-start) | copy-done | bytes 1048600
  1.9 0.0 copy-start.1
  1.9 1.2 %copy-done.1 = bf16[128,4096]{1,0:T(8,128)(2,1)S(1)} copy-done((bf16[128,4096]{1,0:T(8,128)(2,1)S(1)}, bf16[128,4096]{1,0:T(8,128)(2,1)}, u32[]{:S(2)}) %copy-start.1) | copy-done | bytes 1048600
  3.1 0.0 copy-start.2
  3.1 1.2 %copy-done.2 = bf16[128,4096]{1,0:T(8,128)(2,1)S(1)} copy-done((bf16[128,4096]{1,0:T(8,128)(2,1)S(1)}, bf16[128,4096]{1,0:T(8,128)(2,1)}, u32[]{:S(2)}) %copy-start.2) | copy-done | bytes 1048600
  4.3 0.0 copy-start.3
  4.3 1.2 %copy-done.3 = bf16[128,4096]{1,0:T(8,128)(2,1)S(1)} copy-done((bf16[128,4096]{1,0:T(8,128)(2,1)S(1)}, bf16[128,4096]{1,0:T(8,128)(2,1)}, u32[]{:S(2)}) %copy-start.3) | copy-done | bytes 1048600
  5.6 0.0 copy-start.4
  5.6 0.9 %copy-done.4 = bf16[256,512]{1,0:T(8,128)(2,1)S(1)} copy-done((bf16[256,512]{1,0:T(8,128)(2,1)S(1)}, bf16[256,512]{1,0:T(8,128)(2,1)}, u32[]{:S(2)}) %copy-start.4) | copy-done | bytes 262168
  6.5 0.0 copy-start.5
  6.5 0.7 %copy-done.5 = f32[7,256]{1,0:T(8,128)S(1)} copy-done((f32[7,256]{1,0:T(8,128)S(1)}, f32[7,256]{1,0:T(8,128)}, u32[]{:S(2)}) %copy-start.5) | copy-done | bytes 7192
  7.2 39.7 %shard_map.73 = bf16[128,4096]{1,0:T(8,128)(2,1)S(1)} custom-call(bf16[128,4096]{1,0:T(8,128)(2,1)S(1)} %copy-done, bf16[128,4096]{1,0:T(8,128)(2,1)S(1)} %copy-done.1, bf16[128,4096]{1,0:T(8,128)(2,1)S(1)} %copy-done.2, bf16[128,4096]{1,0:T(8,128)(2,1)S(1)} %copy-done.3, s32[1,128]{1,0:T(1,128)S(1)} %bitcast.1, f32[7,256]{1,0:T(8,128)S(1)} %copy-done.5, ...), custom_call_target="tpu_custom_call" | custom-call | tf_op jit(solution)/shard_map/pallas_call | solution.py:398
  46.9 1.0 %copy.9 = bf16[128,4096]{1,0:T(8,128)(2,1)} copy(bf16[128,4096]{1,0:T(8,128)(2,1)S(1)} %shard_map.73) | data formatting | bytes 2097152
Async XLA Ops:
  0.0 0.7 %copy-start.6 = (s32[128]{0:T(128)S(1)}, s32[128]{0:T(128)}, u32[]{:S(2)}) copy-start(s32[128]{0:T(128)} %param.11) | copy-start | bytes 1540
  0.7 1.2 %copy-start = (bf16[128,4096]{1,0:T(8,128)(2,1)S(1)}, bf16[128,4096]{1,0:T(8,128)(2,1)}, u32[]{:S(2)}) copy-start(bf16[128,4096]{1,0:T(8,128)(2,1)} %gs_hbm.1) | copy-start | bytes 3145732
  1.9 1.2 %copy-start.1 = (bf16[128,4096]{1,0:T(8,128)(2,1)S(1)}, bf16[128,4096]{1,0:T(8,128)(2,1)}, u32[]{:S(2)}) copy-start(bf16[128,4096]{1,0:T(8,128)(2,1)} %k_hbm.1) | copy-start | bytes 3145732
  3.1 1.2 %copy-start.2 = (bf16[128,4096]{1,0:T(8,128)(2,1)S(1)}, bf16[128,4096]{1,0:T(8,128)(2,1)}, u32[]{:S(2)}) copy-start(bf16[128,4096]{1,0:T(8,128)(2,1)} %v_hbm.1) | copy-start | bytes 3145732
  4.3 1.2 %copy-start.3 = (bf16[128,4096]{1,0:T(8,128)(2,1)S(1)}, bf16[128,4096]{1,0:T(8,128)(2,1)}, u32[]{:S(2)}) copy-start(bf16[128,4096]{1,0:T(8,128)(2,1)} %gl_hbm.1) | copy-start | bytes 3145732
  5.6 0.9 %copy-start.4 = (bf16[256,512]{1,0:T(8,128)(2,1)S(1)}, bf16[256,512]{1,0:T(8,128)(2,1)}, u32[]{:S(2)}) copy-start(bf16[256,512]{1,0:T(8,128)(2,1)} %h_hbm.1) | copy-start | bytes 786436
  6.5 0.7 %copy-start.5 = (f32[7,256]{1,0:T(8,128)S(1)}, f32[7,256]{1,0:T(8,128)}, u32[]{:S(2)}) copy-start(f32[7,256]{1,0:T(8,128)} %se_hbm.1) | copy-start | bytes 21508

commit v2 on v1

--- a/solution.py
+++ b/solution.py
@@ -13,9 +13,9 @@
 LANES = 128
 PACK = 16
 MSGS = 16
-EARLY = 2
+EARLY = 3
 LAG1 = 2
-LAG2 = 5
+LAG2 = 6
 BASE = 32
 MESH = pl.DeviceIdType.MESH
 
@@ -24,7 +24,7 @@
     count, gs_hbm, k_hbm, v_hbm, gl_hbm, doc_hbm, se_hbm, h_hbm, out_ref,
     gs_ref, k_ref, v_ref, gl_ref, doc_ref, se_ref, h_ref, tail_k, tail_v,
     own, got, doc_out, got_doc, rim_out, rim_in, se_two, doc_ext, ext, agree,
-    rev, taps, acc, near_mask, far_mask, out_mask,
+    rev, taps, acc, near_mask, far_mask, out_mask, ring_all,
     in_sem, one_sem, send_sem, recv_sem, head_send, head_recv, doc_send, doc_recv, rim_send, rim_recv,
 ):
     rows, chans = gs_ref.shape
@@ -46,6 +46,8 @@
     row_mate = me + 2 - 4 * upper
     has_prev = me >= REACH
     has_next = me + REACH < count
+    core_filled = has_prev | (core == 1)
+    row_filled = has_prev | (upper == 1)
 
     def local(src, dst, sem):
         return pltpu.make_async_copy(src, dst, sem)
@@ -64,12 +66,13 @@
     h_in = local(h_hbm, h_ref, one_sem.at[4])
     gl_in = local(gl_hbm, gl_ref, one_sem.at[5])
 
+    for i in range(2):
+        piece(i, 0).start()
+    se_in.start()
+    piece(2, 0).start()
     doc_in.start()
     tails[0].start()
     tails[1].start()
-    se_in.start()
-    for i in range(3):
-        piece(i, 0).start()
 
     barrier = pltpu.get_barrier_semaphore()
 
@@ -103,8 +106,6 @@
     tails[1].wait()
     rim_out[...] = (tail_k[...].astype(f32) * tail_v[...].astype(f32)).astype(bf16)
 
-    pl.semaphore_wait(barrier, peers)
-
     def remote(src, dst, ssem, rsem, target):
         return pltpu.make_async_remote_copy(
             src_ref=src, dst_ref=dst, send_sem=ssem, recv_sem=rsem,
@@ -118,10 +119,6 @@
         slot = REACH - d
         return remote(doc_out, got_doc.at[slot], doc_send.at[slot], doc_recv.at[slot], target)
 
-    pl.when(me + 1 < count)(lambda: rim_copy(me + 1).start())
-    for d in range(1, REACH + 1):
-        pl.when(me + d < count)(lambda d=d: doc_copy(d, me + d).start())
-
     def msg_copy(slot, m, source, target):
         block = own if source is None else got.at[source]
         part = (pl.ds(m * each, each), pl.ds(RIM, body_rows))
@@ -162,9 +159,12 @@
         lanes = lanes_of(ct)
         return (k_ref[part, lanes].astype(f32) * v_ref[part, lanes].astype(f32)).astype(bf16).astype(f32)
 
-    def short_body(j, _):
+    def await_piece(j, _):
         for i in range(3):
             piece(i, j).wait()
+        return 0
+
+    def short_body(j, _):
         for u in range(each):
             ct = j * each + u
             weights = weights_of(ct)
@@ -176,10 +176,35 @@
                 total = total + (shifted * agree[tap, RIM:, :]) * weights[tap : tap + 1, :]
             mixed = gs_ref[RIM:, lanes_of(ct)].astype(f32) * total
             own[ct, RIM:, :] = mixed.astype(bf16)
-        pl.when(j < EARLY)(lambda: send_own(msg(j)))
-        return 0
-
-    lax.fori_loop(0, MSGS, short_body, 0)
+        return 0
+
+    def early_body(j, _):
+        await_piece(j, 0)
+        return short_body(j, 0)
+
+    lax.fori_loop(0, EARLY, early_body, 0)
+
+    pl.semaphore_wait(barrier, peers)
+    pl.when(me + 1 < count)(lambda: rim_copy(me + 1).start())
+    for d in range(1, REACH + 1):
+        pl.when(me + d < count)(lambda d=d: doc_copy(d, me + d).start())
+
+    def send_msg(j, _):
+        send_own(msg(j))
+        return 0
+
+    lax.fori_loop(0, EARLY, send_msg, 0)
+
+
+    def clear(slot):
+        got[slot] = jnp.zeros(got.shape[1:], bf16)
+
+    @pl.when(jnp.logical_not(has_prev))
+    def _():
+        clear(0)
+        pl.when(core == 0)(lambda: clear(1))
+        pl.when(upper == 0)(lambda: clear(2))
+        pl.when(upper == 0)(lambda: clear(3))
 
     h_in.wait()
     lag = lax.broadcasted_iota(i32, (LANES, LANES), 0)
@@ -222,6 +247,8 @@
 
     for tap in range(1, tap_count):
         agree[tap, 0:RIM, :] = (doc_ext[RIM - tap : 2 * RIM - tap, :] == doc_col[0:RIM]).astype(f32)
+
+    lax.fori_loop(EARLY, MSGS, await_piece, 0)
 
     def short_head(j, _):
         for u in range(4):
@@ -241,16 +268,6 @@
     lax.fori_loop(0, tiles // 4, short_head, 0)
     send_own(head_copy)
 
-    def send_rest(j, _):
-        send_own(msg(j))
-        return 0
-
-    lax.fori_loop(EARLY, MSGS, send_rest, 0)
-
-    @pl.when(jnp.logical_not(has_prev))
-    def _():
-        got[0] = jnp.zeros(got.shape[1:], bf16)
-
     gl_in.wait()
 
     tile_group = lax.broadcasted_iota(i32, (1, LANES), 1) // fgroup
@@ -265,16 +282,17 @@
 
     below = [lane[0:PACK] <= row[0:PACK] + r * PACK for r in range(BASE // PACK)]
 
-    def prepare(ct):
+    def prepare(ct, ring_rows):
         first = pl.multiple_of(ct * per_tile, per_tile)
         filt = rev[pl.ds(first, per_tile), :]
+        for d in range(REACH):
+            line = filt[:, d * LANES : (d + 1) * LANES]
+            for i in range(PACK):
+                ring_rows[d, pl.ds(i, per_tile, stride=PACK), :] = line if i == 0 else pltpu.roll(line, i, 1)
         zero = jnp.zeros((PACK, LANES), bf16)
         near = []
         for g in range(per_tile):
-            ring = []
-            for d in range(REACH):
-                line = jnp.broadcast_to(filt[g : g + 1, d * LANES : (d + 1) * LANES], (PACK, LANES))
-                ring.append(pltpu.roll(line, 0, 1, stride=1, stride_axis=0).astype(bf16))
+            ring = [ring_rows[d, g * PACK : (g + 1) * PACK, :].astype(bf16) for d in range(REACH)]
             for r in range(BASE // PACK):
                 turned = ring if r == 0 else [pltpu.roll(c, r * PACK, 1) for c in ring]
                 at_row = g * BASE + r * PACK
@@ -330,15 +348,20 @@
         out_ref[:, lanes_of(ct)] = (gl_ref[:, lanes_of(ct)].astype(f32) * total).astype(bf16)
 
     def step(s, _):
+        @pl.when(s < MSGS - EARLY)
+        def _():
+            short_body(s + EARLY, 0)
+            send_own(msg(s + EARLY))
+
         @pl.when(s < MSGS)
         def _():
             for u in range(each):
-                prepare(s * each + u)
+                prepare(s * each + u, ring_all.at[u])
 
             def relay(copy):
                 pl.when(has_prev)(lambda: copy(0, None, core_mate).wait_recv())
-                pl.when(upper == 1)(lambda: copy(2, 0, row_mate).start())
-                pl.when(core == 1)(lambda: copy(1, 0, core_mate).start())
+                pl.when(has_prev & (upper == 1))(lambda: copy(2, 0, row_mate).start())
+                pl.when(has_prev & (core == 1))(lambda: copy(1, 0, core_mate).start())
 
             pl.when(s == EARLY)(lambda: relay(head_copy))
             relay(msg(s))
@@ -346,8 +369,8 @@
         @pl.when((s >= LAG1) & (s < MSGS + LAG1))
         def _():
             def relay(copy):
-                copy(2, None, core_mate).wait_recv()
-                copy(3, 2, core_mate).start()
+                pl.when(row_filled)(lambda: copy(2, None, core_mate).wait_recv())
+                pl.when(row_filled)(lambda: copy(3, 2, core_mate).start())
 
             pl.when(s == EARLY + LAG1)(lambda: relay(head_copy))
             relay(msg(s - LAG1))
@@ -355,8 +378,8 @@
         @pl.when(s >= LAG2)
         def _():
             def arrive(copy):
-                copy(1, None, core_mate).wait_recv()
-                copy(3, None, core_mate).wait_recv()
+                pl.when(core_filled)(lambda: copy(1, None, core_mate).wait_recv())
+                pl.when(row_filled)(lambda: copy(3, None, core_mate).wait_recv())
 
             pl.when(s == LAG2)(lambda: arrive(head_copy))
             arrive(msg(s - LAG2))
@@ -369,8 +392,9 @@
 
     def drain_all(copy):
         pl.when(has_next)(lambda: copy(0, None, core_mate).wait_send())
-        for slot in (1, 2, 3):
-            copy(slot, None, core_mate).wait_send()
+        pl.when(has_prev | (core == 0))(lambda: copy(1, None, core_mate).wait_send())
+        pl.when(has_prev | (upper == 0))(lambda: copy(2, None, core_mate).wait_send())
+        pl.when(row_filled)(lambda: copy(3, None, core_mate).wait_send())
 
     def drain(j, _):
         drain_all(msg(j))
@@ -397,7 +421,7 @@
     dma = pltpu.SemaphoreType.DMA
     return pl.pallas_call(
         functools.partial(kernel, count),
-        out_shape=jax.ShapeDtypeStruct((rows, chans), bf16),
+        out_shape=pltpu.VMEM((rows, chans), bf16),
         in_specs=[anywhere] * 7,
         out_specs=pl.BlockSpec(memory_space=pltpu.VMEM),
         scratch_shapes=[
@@ -426,6 +450,7 @@
             pltpu.VMEM((2, rows // 2, LANES), bf16),
             pltpu.VMEM((REACH, rows, LANES), bf16),
             pltpu.VMEM((rows, LANES), f32),
+            pltpu.VMEM((tiles // MSGS, REACH, LANES // fgroup * PACK, LANES), f32),
             dma((3, MSGS)),
             dma((6,)),
             dma((REACH, MSGS)),
@@ -438,9 +463,12 @@
             dma,
         ],
         compiler_params=pltpu.CompilerParams(
-            collective_id=0, has_side_effects=True, vmem_limit_bytes=40 * 1024 * 1024
+            collective_id=0, has_side_effects=True, vmem_limit_bytes=48 * 1024 * 1024
         ),
-    )(gate_short, key_short, value_short, gate_long, doc_ids.reshape(1, rows), se_filter, long_filter)
+    )(*(
+        pltpu.with_memory_space_constraint(x, pltpu.HBM)
+        for x in (gate_short, key_short, value_short, gate_long, doc_ids.reshape(1, rows), se_filter, long_filter)
+    ))
 
 
 def solution(mesh):

time: 48.2 us -> 37 us (0.77)
  the two profiles are of different devices: /device:TPU:0 before, /device:TPU:10 now
where the time goes in v2:
time: 37 us; the launch traced here: 36.9 us
  Pallas kernels  35.9 us (97%)
  local copies, waits for them, and re-layouts  0.97 us (3%)
    pallas_call x1, Pallas kernels, body(): pl.pallas_call(functools.partial(kernel, count), out_shape=pltpu.VMEM((ro...  35.9 us
    unnamed x1, local copies, waits for them, and re-layouts  0.97 us

profile of v2, /device:TPU:10, one launch (start us, length us, event | category | flops | bytes accessed | tf_op | source)
XLA Modules:
  0.0 36.9 jit_solution(6917403781946733187)
XLA Ops:
  0.0 35.9 %shard_map.73 = bf16[128,4096]{1,0:T(8,128)(2,1)S(1)} custom-call(bf16[128,4096]{1,0:T(8,128)(2,1)} %gs_hbm.1, bf16[128,4096]{1,0:T(8,128)(2,1)} %k_hbm.1, bf16[128,4096]{1,0:T(8,128)(2,1)} %v_hbm.1, bf16[128,4096]{1,0:T(8,128)(2,1)} %gl_hbm.1, s32[1,128]{1,0:T(1,128)} %bitcast.1, f32[7,256]{1,0:T(8,128)} %se_hbm.1, bf16[256,512]{1,0:T(8,128)(2,1)} %h_hbm.1), custom_call_target="tpu_custom_call" | custom-call | tf_op jit(solution)/shard_map/pallas_call | solution.py:422
  35.9 1.0 %copy.9 = bf16[128,4096]{1,0:T(8,128)(2,1)} copy(bf16[128,4096]{1,0:T(8,128)(2,1)S(1)} %shard_map.73) | data formatting | bytes 2097152

commit v3 on v2

--- a/solution.py
+++ b/solution.py
@@ -15,7 +15,8 @@
 MSGS = 16
 EARLY = 3
 LAG1 = 2
-LAG2 = 6
+LAG2 = 4
+VIA = 2
 BASE = 32
 MESH = pl.DeviceIdType.MESH
 
@@ -24,8 +25,9 @@
     count, gs_hbm, k_hbm, v_hbm, gl_hbm, doc_hbm, se_hbm, h_hbm, out_ref,
     gs_ref, k_ref, v_ref, gl_ref, doc_ref, se_ref, h_ref, tail_k, tail_v,
     own, got, doc_out, got_doc, rim_out, rim_in, se_two, doc_ext, ext, agree,
-    rev, taps, acc, near_mask, far_mask, out_mask, ring_all,
+    rev, taps, acc, near_mask, pair_mask, out_mask, doc_all, ring_all, via,
     in_sem, one_sem, send_sem, recv_sem, head_send, head_recv, doc_send, doc_recv, rim_send, rim_recv,
+    via_send, via_recv, fwd_send,
 ):
     rows, chans = gs_ref.shape
     tap_count, filters = se_ref.shape
@@ -35,6 +37,7 @@
     each = tiles // MSGS
     width = each * LANES
     half = rows // 2
+    direct = MSGS - VIA
     body_rows = rows - RIM
     f32, bf16, i32 = jnp.float32, jnp.bfloat16, jnp.int32
 
@@ -183,6 +186,7 @@
         return short_body(j, 0)
 
     lax.fori_loop(0, EARLY, early_body, 0)
+    lax.fori_loop(direct, MSGS, early_body, 0)
 
     pl.semaphore_wait(barrier, peers)
     pl.when(me + 1 < count)(lambda: rim_copy(me + 1).start())
@@ -193,6 +197,20 @@
         send_own(msg(j))
         return 0
 
+    def side(i):
+        return pl.ds(i * each, each), pl.ds(RIM, body_rows)
+
+    def via_copy(i, target):
+        block = own.at[pl.ds((direct + i) * each, each), pl.ds(RIM, body_rows)]
+        return remote(block, via.at[side(i)], via_send.at[i], via_recv.at[i], target)
+
+    def fwd_copy(i, target):
+        m = direct + i
+        block = got.at[2, pl.ds(m * each, each), pl.ds(RIM, body_rows)]
+        return remote(via.at[side(i)], block, fwd_send.at[i], recv_sem.at[2, m], target)
+
+    for i in range(VIA):
+        pl.when((upper == 1) & has_next)(lambda i=i: via_copy(i, row_mate).start())
     lax.fori_loop(0, EARLY, send_msg, 0)
 
 
@@ -214,17 +232,6 @@
         cols = slice(d * LANES, (d + 1) * LANES)
         rev[:, cols] = jnp.dot(h_ref[:, cols], flip, preferred_element_type=f32)
 
-    low = lane[:half] < half
-    causal = lane[:half] <= row[:half]
-    same_low = doc_col[:half] == doc_row[:half]
-    same_high = doc_col[half:] == pltpu.roll(doc_row[:half], half, 1)
-    late = same_high.astype(f32)
-    early = causal.astype(f32) * same_low.astype(f32)
-    near_mask[0] = jnp.where(low, early, late).astype(bf16)
-    near_mask[1] = jnp.where(low, causal.astype(f32) * late, 0.0).astype(bf16)
-    leader = jnp.broadcast_to(doc_row[0:1, 0:1], (rows, LANES))
-    out_mask[...] = (doc_col == leader).astype(f32)
-
     for w in range(REACH):
         pl.when(me >= REACH - w)(lambda w=w: doc_copy(REACH - w, core_mate).wait_recv())
 
@@ -233,9 +240,32 @@
             got_doc[w] = jnp.full((8, LANES), -1.0, f32)
 
         source_col = jnp.broadcast_to(got_doc[w, 0:1, :], (rows, LANES)).T
-        far_mask[w] = (source_col == leader).astype(bf16)
+        doc_all[w * rows : (w + 1) * rows, :] = source_col
         if w == REACH - 1:
             doc_ext[0:RIM, :] = source_col[rows - RIM :]
+    doc_all[MAXDOC:, :] = doc_col
+
+    windows = rows // BASE
+    low = lane < half
+    leaders = [jnp.broadcast_to(doc_col[a * BASE : a * BASE + 1, :], (MAXDOC, LANES)) for a in range(windows)]
+
+    def matches(a):
+        same = doc_all[a * BASE : a * BASE + MAXDOC, :] == leaders[a]
+        return same.astype(f32)
+
+    def matched(a):
+        same = doc_col[a * BASE : (a + 1) * BASE] == leaders[a][:BASE]
+        return same.astype(f32)
+
+    low_tall = lax.broadcasted_iota(i32, (MAXDOC, LANES), 1) < half
+    block_doc = doc_col[0:BASE]
+    for a in range(1, windows):
+        block_doc = jnp.where(lane[:BASE] // BASE == a, doc_col[a * BASE : (a + 1) * BASE], block_doc)
+    causal = (lax.rem(lane[:BASE], BASE) <= row[:BASE]).astype(f32)
+    near_mask[...] = (causal * (block_doc == doc_row[:BASE]).astype(f32)).astype(bf16)
+    for p in range(windows // 2):
+        pair_mask[p] = jnp.where(low_tall, matches(2 * p), matches(2 * p + 1)).astype(bf16)
+        out_mask[p] = jnp.where(low[:BASE], matched(2 * p), matched(2 * p + 1))
 
     @pl.when(me == 0)
     def _():
@@ -248,7 +278,7 @@
     for tap in range(1, tap_count):
         agree[tap, 0:RIM, :] = (doc_ext[RIM - tap : 2 * RIM - tap, :] == doc_col[0:RIM]).astype(f32)
 
-    lax.fori_loop(EARLY, MSGS, await_piece, 0)
+    lax.fori_loop(EARLY, direct, await_piece, 0)
 
     def short_head(j, _):
         for u in range(4):
@@ -268,6 +298,12 @@
     lax.fori_loop(0, tiles // 4, short_head, 0)
     send_own(head_copy)
 
+    @pl.when((upper == 0) & has_next)
+    def _():
+        for i in range(VIA):
+            via_copy(i, row_mate).wait_recv()
+            fwd_copy(i, me + REACH).start()
+
     gl_in.wait()
 
     tile_group = lax.broadcasted_iota(i32, (1, LANES), 1) // fgroup
@@ -281,6 +317,9 @@
         return picked
 
     below = [lane[0:PACK] <= row[0:PACK] + r * PACK for r in range(BASE // PACK)]
+
+    place = lax.rem(lane[0:PACK] + PACK, LANES) // BASE
+    arc = [place == b for b in range(rows // BASE)]
 
     def prepare(ct, ring_rows):
         first = pl.multiple_of(ct * per_tile, per_tile)
@@ -290,6 +329,7 @@
             for i in range(PACK):
                 ring_rows[d, pl.ds(i, per_tile, stride=PACK), :] = line if i == 0 else pltpu.roll(line, i, 1)
         zero = jnp.zeros((PACK, LANES), bf16)
+        zero_base = jnp.zeros((BASE, LANES), bf16)
         near = []
         for g in range(per_tile):
             ring = [ring_rows[d, g * PACK : (g + 1) * PACK, :].astype(bf16) for d in range(REACH)]
@@ -300,23 +340,37 @@
                     d = REACH - w
                     recent = turned[d] if d < REACH else zero
                     taps[ct, w, at_row : at_row + PACK, :] = jnp.where(below[r], recent, turned[d - 1])
-            for r in range(half // PACK):
-                turned = ring[0] if r == 0 else pltpu.roll(ring[0], r * PACK, 1)
-                at_mask = slice(r * PACK, (r + 1) * PACK)
-                near.append(jnp.concatenate([turned * near_mask[0, at_mask], turned * near_mask[1, at_mask]], 1))
+            around = ring[0]
+            for b in range(1, rows // BASE):
+                around = jnp.where(arc[b], pltpu.roll(ring[0], b * BASE, 1), around)
+            for r in range(BASE // PACK):
+                turned = around if r == 0 else pltpu.roll(around, r * PACK, 1)
+                near.append(turned * near_mask[r * PACK : (r + 1) * PACK])
         block = own[ct]
-        first_half, second_half = block[:half], block[half:]
+        turned = pltpu.roll(block, half, 1)
         none = jnp.zeros((half, LANES), bf16)
-        right = jnp.concatenate(
-            [
-                jnp.concatenate([first_half, none, none, none], 0),
-                jnp.concatenate([none, first_half, second_half, none], 0),
-            ],
-            1,
-        )
-        result = jnp.dot(jnp.concatenate(near, 0), right, preferred_element_type=f32)
-        acc[ct, 0:half, :] = pick(result, tile_group, per_tile, half, slice(0, LANES))
-        acc[ct, half:, :] = pick(result, tile_group, per_tile, half, slice(LANES, 2 * LANES))
+        for h in range(2):
+            first, second = (block, turned) if h == 0 else (turned, block)
+            spread_out = jnp.concatenate(
+                [
+                    jnp.where(low_half, first[a * BASE : (a + 1) * BASE], zero_base)
+                    if a % 2 == 0
+                    else jnp.where(low_half, zero_base, second[a * BASE : (a + 1) * BASE])
+                    for a in range(rows // BASE)
+                ],
+                0,
+            )
+            right = jnp.concatenate(
+                [jnp.concatenate([spread_out[:half], none], 0), jnp.concatenate([none, spread_out[half:]], 0)], 1
+            )
+            count_near = per_tile // 2 * (BASE // PACK)
+            lhs = jnp.concatenate(near[h * count_near : (h + 1) * count_near], 0)
+            result = jnp.dot(lhs, right, preferred_element_type=f32)
+            for p in range(2):
+                at_row = (2 * h + p) * BASE
+                acc[ct, at_row : at_row + BASE, :] = pick(
+                    result, half_group, per_tile // 2, BASE, slice(p * LANES, (p + 1) * LANES)
+                )
 
     slots = []
     for w in range(REACH):
@@ -324,47 +378,59 @@
         slots.append(lax.rem(q // 2 + upper, 2) * 2 + lax.rem(q + at, 2))
 
     def far(ct):
-        left = jnp.concatenate([got[slots[w], ct] * far_mask[w] for w in range(REACH)], 0)
-        gap = jnp.zeros((BASE, LANES), bf16)
-        later = jnp.concatenate([left[BASE:], gap], 0)
+        reach = [got[slots[w], ct] for w in range(REACH)] + [own[ct, 0 : rows - BASE, :]]
+        source = jnp.concatenate(reach, 0)
+        turned = pltpu.roll(source, half, 1)
+        tall = MAXDOC + half
         outs = []
         for h in range(2):
-            if h == 0:
-                pair = jnp.where(low_half, left, pltpu.roll(later, half, 1))
-            else:
-                pair = jnp.where(low_half, pltpu.roll(left, half, 1), later)
-            wide = jnp.concatenate([pair, jnp.concatenate([pair[2 * BASE :], gap, gap], 0)], 1)
+            first, second = (source, turned) if h == 0 else (turned, source)
+            pair = jnp.where(low_half, first[:tall], second[BASE : BASE + tall])
+            wide = jnp.concatenate([pair[p * half : p * half + MAXDOC] * pair_mask[p] for p in range(2)], 1)
             height = per_tile // 2 * BASE
             lhs = jnp.concatenate([taps[ct, w, h * height : (h + 1) * height, :] for w in range(REACH)], 1)
             result = jnp.dot(lhs, wide, preferred_element_type=f32)
-            outs.append(
-                [pick(result, half_group, per_tile // 2, BASE, slice(p * LANES, (p + 1) * LANES)) for p in range(2)]
-            )
+            total = []
+            for p in range(2):
+                picked = pick(result, half_group, per_tile // 2, BASE, slice(p * LANES, (p + 1) * LANES))
+                at_row = (2 * h + p) * BASE
+                total.append(acc[ct, at_row : at_row + BASE, :] + picked * out_mask[p])
+            outs.append(total)
         both = []
         for p in range(2):
             both.append(jnp.where(low_half, outs[0][p], pltpu.roll(outs[1][p], half, 1)))
             both.append(jnp.where(low_half, pltpu.roll(outs[0][p], half, 1), outs[1][p]))
-        total = acc[ct] + jnp.concatenate(both, 0) * out_mask[...]
+        total = jnp.concatenate(both, 0)
         out_ref[:, lanes_of(ct)] = (gl_ref[:, lanes_of(ct)].astype(f32) * total).astype(bf16)
 
     def step(s, _):
         @pl.when(s < MSGS - EARLY)
         def _():
-            short_body(s + EARLY, 0)
+            @pl.when(s < direct - EARLY)
+            def _():
+                short_body(s + EARLY, 0)
+
             send_own(msg(s + EARLY))
+
+        def prepare_msg(m, _):
+            for u in range(each):
+                prepare(m * each + u, ring_all.at[u])
+            return 0
+
+        def prepared(s):
+            return jnp.minimum(jnp.minimum(2 * s, s + EARLY), MSGS)
+
+        lax.fori_loop(prepared(s), prepared(s + 1), prepare_msg, 0)
 
         @pl.when(s < MSGS)
         def _():
-            for u in range(each):
-                prepare(s * each + u, ring_all.at[u])
-
-            def relay(copy):
+            def relay(copy, row_too=True):
                 pl.when(has_prev)(lambda: copy(0, None, core_mate).wait_recv())
-                pl.when(has_prev & (upper == 1))(lambda: copy(2, 0, row_mate).start())
+                pl.when(has_prev & (upper == 1) & row_too)(lambda: copy(2, 0, row_mate).start())
                 pl.when(has_prev & (core == 1))(lambda: copy(1, 0, core_mate).start())
 
             pl.when(s == EARLY)(lambda: relay(head_copy))
-            relay(msg(s))
+            relay(msg(s), s < direct)
 
         @pl.when((s >= LAG1) & (s < MSGS + LAG1))
         def _():
@@ -375,33 +441,41 @@
             pl.when(s == EARLY + LAG1)(lambda: relay(head_copy))
             relay(msg(s - LAG1))
 
-        @pl.when(s >= LAG2)
-        def _():
+        def finished(s):
+            ahead = jnp.maximum(s - (EARLY + LAG1 + 1), 0)
+            return jnp.minimum(jnp.minimum(ahead + ahead // 3, jnp.maximum(s - LAG2, 0)), MSGS)
+
+        def far_msg(m, _):
             def arrive(copy):
                 pl.when(core_filled)(lambda: copy(1, None, core_mate).wait_recv())
                 pl.when(row_filled)(lambda: copy(3, None, core_mate).wait_recv())
 
-            pl.when(s == LAG2)(lambda: arrive(head_copy))
-            arrive(msg(s - LAG2))
+            pl.when(m == 0)(lambda: arrive(head_copy))
+            arrive(msg(m))
             for u in range(each):
-                far((s - LAG2) * each + u)
-
+                far(m * each + u)
+            return 0
+
+        lax.fori_loop(finished(s), finished(s + 1), far_msg, 0)
         return 0
 
     lax.fori_loop(0, MSGS + LAG2, step, 0)
 
-    def drain_all(copy):
+    def drain_all(copy, row_too=True):
         pl.when(has_next)(lambda: copy(0, None, core_mate).wait_send())
         pl.when(has_prev | (core == 0))(lambda: copy(1, None, core_mate).wait_send())
-        pl.when(has_prev | (upper == 0))(lambda: copy(2, None, core_mate).wait_send())
+        pl.when((has_prev & row_too) | (upper == 0))(lambda: copy(2, None, core_mate).wait_send())
         pl.when(row_filled)(lambda: copy(3, None, core_mate).wait_send())
 
     def drain(j, _):
-        drain_all(msg(j))
+        drain_all(msg(j), j < direct)
         return 0
 
     lax.fori_loop(0, MSGS, drain, 0)
     drain_all(head_copy)
+    for i in range(VIA):
+        pl.when((upper == 1) & has_next)(lambda i=i: via_copy(i, core_mate).wait_send())
+        pl.when((upper == 0) & has_next)(lambda i=i: fwd_copy(i, core_mate).wait_send())
     pl.when(me + 1 < count)(lambda: rim_copy(core_mate).wait_send())
     for d in range(1, REACH + 1):
         pl.when(me + d < count)(lambda d=d: doc_copy(d, core_mate).wait_send())
@@ -447,10 +521,12 @@
             pltpu.VMEM((filters, MAXDOC), f32),
             pltpu.VMEM((tiles, REACH, LANES // fgroup * BASE, LANES), bf16),
             pltpu.VMEM((tiles, rows, LANES), f32),
-            pltpu.VMEM((2, rows // 2, LANES), bf16),
-            pltpu.VMEM((REACH, rows, LANES), bf16),
-            pltpu.VMEM((rows, LANES), f32),
+            pltpu.VMEM((BASE, LANES), bf16),
+            pltpu.VMEM((rows // BASE // 2, MAXDOC, LANES), bf16),
+            pltpu.VMEM((rows // BASE // 2, BASE, LANES), f32),
+            pltpu.VMEM((MAXDOC + rows, LANES), f32),
             pltpu.VMEM((tiles // MSGS, REACH, LANES // fgroup * PACK, LANES), f32),
+            pltpu.VMEM((VIA * (tiles // MSGS), rows, LANES), bf16),
             dma((3, MSGS)),
             dma((6,)),
             dma((REACH, MSGS)),
@@ -461,6 +537,9 @@
             dma((REACH,)),
             dma,
             dma,
+            dma((VIA,)),
+            dma((VIA,)),
+            dma((VIA,)),
         ],
         compiler_params=pltpu.CompilerParams(
             collective_id=0, has_side_effects=True, vmem_limit_bytes=48 * 1024 * 1024

time: 37 us -> 36.4 us (0.984); the launches traced: 36.9 us -> 35.9 us
  Pallas kernels: 35.9 us -> 34.9 us
    pallas_call x1, Pallas kernels: 35.9 us -> 34.9 us  [body(): pl.pallas_call(functools.partial(kernel, count), out_shape=pltpu.VMEM((ro...]
where the time goes in v3:
time: 36.4 us; the launch traced here: 35.9 us
  Pallas kernels  34.9 us (96%)
  local copies, waits for them, and re-layouts  0.97 us (3%)
    pallas_call x1, Pallas kernels, body(): pl.pallas_call(functools.partial(kernel, count), out_shape=pltpu.VMEM((ro...  34.9 us
    unnamed x1, local copies, waits for them, and re-layouts  0.97 us

profile of v3, /device:TPU:10, one launch (start us, length us, event | category | flops | bytes accessed | tf_op | source)
XLA Modules:
  0.0 35.9 jit_solution(3909410135892399492)
XLA Ops:
  0.0 34.9 %shard_map.73 = bf16[128,4096]{1,0:T(8,128)(2,1)S(1)} custom-call(bf16[128,4096]{1,0:T(8,128)(2,1)} %gs_hbm.1, bf16[128,4096]{1,0:T(8,128)(2,1)} %k_hbm.1, bf16[128,4096]{1,0:T(8,128)(2,1)} %v_hbm.1, bf16[128,4096]{1,0:T(8,128)(2,1)} %gl_hbm.1, s32[1,128]{1,0:T(1,128)} %bitcast.1, f32[7,256]{1,0:T(8,128)} %se_hbm.1, bf16[256,512]{1,0:T(8,128)(2,1)} %h_hbm.1), custom_call_target="tpu_custom_call" | custom-call | tf_op jit(solution)/shard_map/pallas_call | solution.py:496
  34.9 1.0 %copy.9 = bf16[128,4096]{1,0:T(8,128)(2,1)} copy(bf16[128,4096]{1,0:T(8,128)(2,1)S(1)} %shard_map.73) | data formatting | bytes 2097152

commit v4 on v2

--- a/solution.py
+++ b/solution.py
@@ -15,7 +15,8 @@
 MSGS = 16
 EARLY = 3
 LAG1 = 2
-LAG2 = 6
+LAG2 = 4
+VIA = 2
 BASE = 32
 MESH = pl.DeviceIdType.MESH
 
@@ -24,8 +25,9 @@
     count, gs_hbm, k_hbm, v_hbm, gl_hbm, doc_hbm, se_hbm, h_hbm, out_ref,
     gs_ref, k_ref, v_ref, gl_ref, doc_ref, se_ref, h_ref, tail_k, tail_v,
     own, got, doc_out, got_doc, rim_out, rim_in, se_two, doc_ext, ext, agree,
-    rev, taps, acc, near_mask, far_mask, out_mask, ring_all,
+    rev, taps, acc, near_mask, far_mask, out_mask, ring_all, via,
     in_sem, one_sem, send_sem, recv_sem, head_send, head_recv, doc_send, doc_recv, rim_send, rim_recv,
+    via_send, via_recv, fwd_send,
 ):
     rows, chans = gs_ref.shape
     tap_count, filters = se_ref.shape
@@ -35,6 +37,7 @@
     each = tiles // MSGS
     width = each * LANES
     half = rows // 2
+    direct = MSGS - VIA
     body_rows = rows - RIM
     f32, bf16, i32 = jnp.float32, jnp.bfloat16, jnp.int32
 
@@ -122,7 +125,7 @@
     def msg_copy(slot, m, source, target):
         block = own if source is None else got.at[source]
         part = (pl.ds(m * each, each), pl.ds(RIM, body_rows))
-        return remote(block.at[part], got.at[(slot, *part)], send_sem.at[slot, m], recv_sem.at[slot, m], target)
+        return remote(block.at[part], got.at[(slot, *part)], send_sem.at[slot], recv_sem.at[slot, m], target)
 
     def head_copy(slot, source, target):
         block = own if source is None else got.at[source]
@@ -183,6 +186,7 @@
         return short_body(j, 0)
 
     lax.fori_loop(0, EARLY, early_body, 0)
+    lax.fori_loop(direct, MSGS, early_body, 0)
 
     pl.semaphore_wait(barrier, peers)
     pl.when(me + 1 < count)(lambda: rim_copy(me + 1).start())
@@ -193,6 +197,20 @@
         send_own(msg(j))
         return 0
 
+    def side(i):
+        return pl.ds(i * each, each), pl.ds(RIM, body_rows)
+
+    def via_copy(i, target):
+        block = own.at[pl.ds((direct + i) * each, each), pl.ds(RIM, body_rows)]
+        return remote(block, via.at[side(i)], via_send.at[i], via_recv.at[i], target)
+
+    def fwd_copy(i, target):
+        m = direct + i
+        block = got.at[2, pl.ds(m * each, each), pl.ds(RIM, body_rows)]
+        return remote(via.at[side(i)], block, fwd_send.at[i], recv_sem.at[2, m], target)
+
+    for i in range(VIA):
+        pl.when((upper == 1) & has_next)(lambda i=i: via_copy(i, row_mate).start())
     lax.fori_loop(0, EARLY, send_msg, 0)
 
 
@@ -248,7 +266,7 @@
     for tap in range(1, tap_count):
         agree[tap, 0:RIM, :] = (doc_ext[RIM - tap : 2 * RIM - tap, :] == doc_col[0:RIM]).astype(f32)
 
-    lax.fori_loop(EARLY, MSGS, await_piece, 0)
+    lax.fori_loop(EARLY, direct, await_piece, 0)
 
     def short_head(j, _):
         for u in range(4):
@@ -267,6 +285,12 @@
 
     lax.fori_loop(0, tiles // 4, short_head, 0)
     send_own(head_copy)
+
+    @pl.when((upper == 0) & has_next)
+    def _():
+        for i in range(VIA):
+            via_copy(i, row_mate).wait_recv()
+            fwd_copy(i, me + REACH).start()
 
     gl_in.wait()
 
@@ -350,21 +374,29 @@
     def step(s, _):
         @pl.when(s < MSGS - EARLY)
         def _():
-            short_body(s + EARLY, 0)
+            @pl.when(s < direct - EARLY)
+            def _():
+                short_body(s + EARLY, 0)
+
             send_own(msg(s + EARLY))
+
+        def prepared(s):
+            return jnp.minimum(jnp.minimum(s, (s + EARLY) // 2), MSGS // 2)
+
+        @pl.when(prepared(s + 1) > prepared(s))
+        def _():
+            for u in range(2 * each):
+                prepare(prepared(s) * (2 * each) + u, ring_all.at[u])
 
         @pl.when(s < MSGS)
         def _():
-            for u in range(each):
-                prepare(s * each + u, ring_all.at[u])
-
-            def relay(copy):
+            def relay(copy, row_too=True):
                 pl.when(has_prev)(lambda: copy(0, None, core_mate).wait_recv())
-                pl.when(has_prev & (upper == 1))(lambda: copy(2, 0, row_mate).start())
+                pl.when(has_prev & (upper == 1) & row_too)(lambda: copy(2, 0, row_mate).start())
                 pl.when(has_prev & (core == 1))(lambda: copy(1, 0, core_mate).start())
 
             pl.when(s == EARLY)(lambda: relay(head_copy))
-            relay(msg(s))
+            relay(msg(s), s < direct)
 
         @pl.when((s >= LAG1) & (s < MSGS + LAG1))
         def _():
@@ -375,33 +407,43 @@
             pl.when(s == EARLY + LAG1)(lambda: relay(head_copy))
             relay(msg(s - LAG1))
 
-        @pl.when(s >= LAG2)
-        def _():
+        def finished(s):
+            paired = (s - LAG2) // 2 * 2
+            done = jnp.where(s <= MSGS, paired, s - LAG2)
+            return jnp.where(s <= EARLY + LAG1 + 1, 0, done)
+
+        def far_msgs(m, many):
             def arrive(copy):
                 pl.when(core_filled)(lambda: copy(1, None, core_mate).wait_recv())
                 pl.when(row_filled)(lambda: copy(3, None, core_mate).wait_recv())
 
-            pl.when(s == LAG2)(lambda: arrive(head_copy))
-            arrive(msg(s - LAG2))
-            for u in range(each):
-                far((s - LAG2) * each + u)
+            pl.when(m == 0)(lambda: arrive(head_copy))
+            for i in range(many):
+                arrive(msg(m + i))
+            for u in range(many * each):
+                far(m * each + u)
+
+        for many in (1, 2):
+            pl.when(finished(s + 1) - finished(s) == many)(lambda many=many: far_msgs(finished(s), many))
 
         return 0
 
     lax.fori_loop(0, MSGS + LAG2, step, 0)
 
-    def drain_all(copy):
-        pl.when(has_next)(lambda: copy(0, None, core_mate).wait_send())
-        pl.when(has_prev | (core == 0))(lambda: copy(1, None, core_mate).wait_send())
-        pl.when(has_prev | (upper == 0))(lambda: copy(2, None, core_mate).wait_send())
-        pl.when(row_filled)(lambda: copy(3, None, core_mate).wait_send())
-
-    def drain(j, _):
-        drain_all(msg(j))
-        return 0
-
-    lax.fori_loop(0, MSGS, drain, 0)
-    drain_all(head_copy)
+    def drain(slot, msgs):
+        part = (pl.ds(0, msgs * each), pl.ds(RIM, body_rows))
+        block = own.at[part]
+        remote(block, got.at[(slot, *part)], send_sem.at[slot], recv_sem.at[slot, 0], core_mate).wait_send()
+        head_copy(slot, None, core_mate).wait_send()
+
+    pl.when(has_next)(lambda: drain(0, MSGS))
+    pl.when(has_prev | (core == 0))(lambda: drain(1, MSGS))
+    pl.when(upper == 0)(lambda: drain(2, MSGS))
+    pl.when(has_prev & (upper == 1))(lambda: drain(2, direct))
+    pl.when(row_filled)(lambda: drain(3, MSGS))
+    for i in range(VIA):
+        pl.when((upper == 1) & has_next)(lambda i=i: via_copy(i, core_mate).wait_send())
+        pl.when((upper == 0) & has_next)(lambda i=i: fwd_copy(i, core_mate).wait_send())
     pl.when(me + 1 < count)(lambda: rim_copy(core_mate).wait_send())
     for d in range(1, REACH + 1):
         pl.when(me + d < count)(lambda d=d: doc_copy(d, core_mate).wait_send())
@@ -450,10 +492,11 @@
             pltpu.VMEM((2, rows // 2, LANES), bf16),
             pltpu.VMEM((REACH, rows, LANES), bf16),
             pltpu.VMEM((rows, LANES), f32),
-            pltpu.VMEM((tiles // MSGS, REACH, LANES // fgroup * PACK, LANES), f32),
+            pltpu.VMEM((2 * (tiles // MSGS), REACH, LANES // fgroup * PACK, LANES), f32),
+            pltpu.VMEM((VIA * (tiles // MSGS), rows, LANES), bf16),
             dma((3, MSGS)),
             dma((6,)),
-            dma((REACH, MSGS)),
+            dma((REACH,)),
             dma((REACH, MSGS)),
             dma((REACH,)),
             dma((REACH,)),
@@ -461,6 +504,9 @@
             dma((REACH,)),
             dma,
             dma,
+            dma((VIA,)),
+            dma((VIA,)),
+            dma((VIA,)),
         ],
         compiler_params=pltpu.CompilerParams(
             collective_id=0, has_side_effects=True, vmem_limit_bytes=48 * 1024 * 1024

time: 37 us -> 35.2 us (0.951)
  Pallas kernels: 35.9 us -> 33.8 us
    pallas_call x1, Pallas kernels: 35.9 us -> 33.8 us  [body(): pl.pallas_call(functools.partial(kernel, count), out_shape=pltpu.VMEM((ro...]
where the time goes in v4:
time: 35.2 us; the launch traced here: 34.7 us
  Pallas kernels  33.8 us (96%)
  local copies, waits for them, and re-layouts  0.97 us (3%)
    pallas_call x1, Pallas kernels, body(): pl.pallas_call(functools.partial(kernel, count), out_shape=pltpu.VMEM((ro...  33.8 us
    unnamed x1, local copies, waits for them, and re-layouts  0.97 us

profile of v4, /device:TPU:10, one launch (start us, length us, event | category | flops | bytes accessed | tf_op | source)
XLA Modules:
  0.0 34.7 jit_solution(12976043526084077253)
XLA Ops:
  0.0 33.8 %shard_map.73 = bf16[128,4096]{1,0:T(8,128)(2,1)S(1)} custom-call(bf16[128,4096]{1,0:T(8,128)(2,1)} %gs_hbm.1, bf16[128,4096]{1,0:T(8,128)(2,1)} %k_hbm.1, bf16[128,4096]{1,0:T(8,128)(2,1)} %v_hbm.1, bf16[128,4096]{1,0:T(8,128)(2,1)} %gl_hbm.1, s32[1,128]{1,0:T(1,128)} %bitcast.1, f32[7,256]{1,0:T(8,128)} %se_hbm.1, bf16[256,512]{1,0:T(8,128)(2,1)} %h_hbm.1), custom_call_target="tpu_custom_call" | custom-call | tf_op jit(solution)/shard_map/pallas_call | solution.py:464
  33.8 1.0 %copy.9 = bf16[128,4096]{1,0:T(8,128)(2,1)} copy(bf16[128,4096]{1,0:T(8,128)(2,1)S(1)} %shard_map.73) | data formatting | bytes 2097152

commit v5 on v4

--- a/solution.py
+++ b/solution.py
@@ -17,6 +17,9 @@
 LAG1 = 2
 LAG2 = 4
 VIA = 2
+GROUPS = 4
+FIRST = 2
+AHEAD = 2
 BASE = 32
 MESH = pl.DeviceIdType.MESH
 
@@ -25,7 +28,7 @@
     count, gs_hbm, k_hbm, v_hbm, gl_hbm, doc_hbm, se_hbm, h_hbm, out_ref,
     gs_ref, k_ref, v_ref, gl_ref, doc_ref, se_ref, h_ref, tail_k, tail_v,
     own, got, doc_out, got_doc, rim_out, rim_in, se_two, doc_ext, ext, agree,
-    rev, taps, acc, near_mask, far_mask, out_mask, ring_all, via,
+    rev, taps, acc, near_mask, far_mask, out_mask, ring_all, close, via,
     in_sem, one_sem, send_sem, recv_sem, head_send, head_recv, doc_send, doc_recv, rim_send, rim_recv,
     via_send, via_recv, fwd_send,
 ):
@@ -57,7 +60,7 @@
 
     def piece(i, j):
         src, dst = ((k_hbm, k_ref), (v_hbm, v_ref), (gs_hbm, gs_ref))[i]
-        cols = pl.ds(pl.multiple_of(j * width, width), width)
+        cols = slice(j * chans // GROUPS, (j + 1) * chans // GROUPS)
         return local(src.at[:, cols], dst.at[:, cols], in_sem.at[i, j])
 
     doc_in = local(doc_hbm, doc_ref, one_sem.at[0])
@@ -88,12 +91,9 @@
         pl.when(me + d < count)(lambda d=d: greet(me + d))
         peers = peers + (me >= d).astype(i32) + (me + d < count).astype(i32)
 
-    def fetch(j, _):
+    for j in (GROUPS - 1, *range(1, GROUPS - 1)):
         for i in range(3):
             piece(i, j).start()
-        return 0
-
-    lax.fori_loop(1, MSGS, fetch, 0)
     h_in.start()
     gl_in.start()
 
@@ -162,10 +162,9 @@
         lanes = lanes_of(ct)
         return (k_ref[part, lanes].astype(f32) * v_ref[part, lanes].astype(f32)).astype(bf16).astype(f32)
 
-    def await_piece(j, _):
+    def await_pieces(j):
         for i in range(3):
             piece(i, j).wait()
-        return 0
 
     def short_body(j, _):
         for u in range(each):
@@ -181,12 +180,8 @@
             own[ct, RIM:, :] = mixed.astype(bf16)
         return 0
 
-    def early_body(j, _):
-        await_piece(j, 0)
-        return short_body(j, 0)
-
-    lax.fori_loop(0, EARLY, early_body, 0)
-    lax.fori_loop(direct, MSGS, early_body, 0)
+    await_pieces(0)
+    lax.fori_loop(0, FIRST, short_body, 0)
 
     pl.semaphore_wait(barrier, peers)
     pl.when(me + 1 < count)(lambda: rim_copy(me + 1).start())
@@ -209,9 +204,12 @@
         block = got.at[2, pl.ds(m * each, each), pl.ds(RIM, body_rows)]
         return remote(via.at[side(i)], block, fwd_send.at[i], recv_sem.at[2, m], target)
 
+    lax.fori_loop(0, FIRST, send_msg, 0)
+    await_pieces(GROUPS - 1)
+    lax.fori_loop(direct, MSGS, short_body, 0)
     for i in range(VIA):
         pl.when((upper == 1) & has_next)(lambda i=i: via_copy(i, row_mate).start())
-    lax.fori_loop(0, EARLY, send_msg, 0)
+    lax.fori_loop(FIRST, EARLY, lambda j, c: send_msg(j, short_body(j, c)), 0)
 
 
     def clear(slot):
@@ -243,6 +241,35 @@
     leader = jnp.broadcast_to(doc_row[0:1, 0:1], (rows, LANES))
     out_mask[...] = (doc_col == leader).astype(f32)
 
+    below = [lane[0:PACK] <= row[0:PACK] + r * PACK for r in range(BASE // PACK)]
+
+    def build_taps(ct, ring_rows):
+        first = pl.multiple_of(ct * per_tile, per_tile)
+        filt = rev[pl.ds(first, per_tile), :]
+        for d in range(REACH):
+            line = filt[:, d * LANES : (d + 1) * LANES]
+            for i in range(PACK):
+                ring_rows[d, pl.ds(i, per_tile, stride=PACK), :] = line if i == 0 else pltpu.roll(line, i, 1)
+        zero = jnp.zeros((PACK, LANES), bf16)
+        for g in range(per_tile):
+            ring = [ring_rows[d, g * PACK : (g + 1) * PACK, :].astype(bf16) for d in range(REACH)]
+            for r in range(BASE // PACK):
+                turned = ring if r == 0 else [pltpu.roll(c, r * PACK, 1) for c in ring]
+                at_row = g * BASE + r * PACK
+                for w in range(REACH):
+                    d = REACH - w
+                    recent = turned[d] if d < REACH else zero
+                    taps[ct, w, at_row : at_row + PACK, :] = jnp.where(below[r], recent, turned[d - 1])
+        return ring_rows[0].astype(bf16)
+
+    def build_ahead(q, _):
+        for u in range(2 * each):
+            ct = q * (2 * each) + u
+            close[ct] = build_taps(ct, ring_all.at[u])
+        return 0
+
+    lax.fori_loop(0, AHEAD, build_ahead, 0)
+
     for w in range(REACH):
         pl.when(me >= REACH - w)(lambda w=w: doc_copy(REACH - w, core_mate).wait_recv())
 
@@ -266,7 +293,8 @@
     for tap in range(1, tap_count):
         agree[tap, 0:RIM, :] = (doc_ext[RIM - tap : 2 * RIM - tap, :] == doc_col[0:RIM]).astype(f32)
 
-    lax.fori_loop(EARLY, direct, await_piece, 0)
+    for j in range(1, GROUPS - 1):
+        await_pieces(j)
 
     def short_head(j, _):
         for u in range(4):
@@ -304,28 +332,12 @@
             picked = jnp.where(group == g, result[g * height : (g + 1) * height, lanes], picked)
         return picked
 
-    below = [lane[0:PACK] <= row[0:PACK] + r * PACK for r in range(BASE // PACK)]
-
-    def prepare(ct, ring_rows):
-        first = pl.multiple_of(ct * per_tile, per_tile)
-        filt = rev[pl.ds(first, per_tile), :]
-        for d in range(REACH):
-            line = filt[:, d * LANES : (d + 1) * LANES]
-            for i in range(PACK):
-                ring_rows[d, pl.ds(i, per_tile, stride=PACK), :] = line if i == 0 else pltpu.roll(line, i, 1)
-        zero = jnp.zeros((PACK, LANES), bf16)
+    def near_part(ct, close_rows):
         near = []
         for g in range(per_tile):
-            ring = [ring_rows[d, g * PACK : (g + 1) * PACK, :].astype(bf16) for d in range(REACH)]
-            for r in range(BASE // PACK):
-                turned = ring if r == 0 else [pltpu.roll(c, r * PACK, 1) for c in ring]
-                at_row = g * BASE + r * PACK
-                for w in range(REACH):
-                    d = REACH - w
-                    recent = turned[d] if d < REACH else zero
-                    taps[ct, w, at_row : at_row + PACK, :] = jnp.where(below[r], recent, turned[d - 1])
+            ring = close_rows[g * PACK : (g + 1) * PACK]
             for r in range(half // PACK):
-                turned = ring[0] if r == 0 else pltpu.roll(ring[0], r * PACK, 1)
+                turned = ring if r == 0 else pltpu.roll(ring, r * PACK, 1)
                 at_mask = slice(r * PACK, (r + 1) * PACK)
                 near.append(jnp.concatenate([turned * near_mask[0, at_mask], turned * near_mask[1, at_mask]], 1))
         block = own[ct]
@@ -383,10 +395,20 @@
         def prepared(s):
             return jnp.minimum(jnp.minimum(s, (s + EARLY) // 2), MSGS // 2)
 
-        @pl.when(prepared(s + 1) > prepared(s))
+        group = prepared(s)
+        fresh = prepared(s + 1) > group
+
+        @pl.when(fresh & (group < AHEAD))
         def _():
             for u in range(2 * each):
-                prepare(prepared(s) * (2 * each) + u, ring_all.at[u])
+                ct = group * (2 * each) + u
+                near_part(ct, close[ct])
+
+        @pl.when(fresh & (group >= AHEAD))
+        def _():
+            for u in range(2 * each):
+                ct = group * (2 * each) + u
+                near_part(ct, build_taps(ct, ring_all.at[u]))
 
         @pl.when(s < MSGS)
         def _():
@@ -493,8 +515,9 @@
             pltpu.VMEM((REACH, rows, LANES), bf16),
             pltpu.VMEM((rows, LANES), f32),
             pltpu.VMEM((2 * (tiles // MSGS), REACH, LANES // fgroup * PACK, LANES), f32),
+            pltpu.VMEM((AHEAD * 2 * (tiles // MSGS), LANES // fgroup * PACK, LANES), bf16),
             pltpu.VMEM((VIA * (tiles // MSGS), rows, LANES), bf16),
-            dma((3, MSGS)),
+            dma((3, GROUPS)),
             dma((6,)),
             dma((REACH,)),
             dma((REACH, MSGS)),

time: 35.2 us -> 33.9 us (0.963)
  Pallas kernels: 33.8 us -> 32.5 us
    pallas_call x1, Pallas kernels: 33.8 us -> 32.5 us  [body(): pl.pallas_call(functools.partial(kernel, count), out_shape=pltpu.VMEM((ro...]
where the time goes in v5:
time: 33.9 us; the launch traced here: 33.4 us
  Pallas kernels  32.5 us (96%)
  local copies, waits for them, and re-layouts  0.97 us (3%)
    pallas_call x1, Pallas kernels, body(): pl.pallas_call(functools.partial(kernel, count), out_shape=pltpu.VMEM((ro...  32.5 us
    unnamed x1, local copies, waits for them, and re-layouts  0.97 us

profile of v5, /device:TPU:10, one launch (start us, length us, event | category | flops | bytes accessed | tf_op | source)
XLA Modules:
  0.0 33.4 jit_solution(3729402562028717654)
XLA Ops:
  0.0 32.5 %shard_map.73 = bf16[128,4096]{1,0:T(8,128)(2,1)S(1)} custom-call(bf16[128,4096]{1,0:T(8,128)(2,1)} %gs_hbm.1, bf16[128,4096]{1,0:T(8,128)(2,1)} %k_hbm.1, bf16[128,4096]{1,0:T(8,128)(2,1)} %v_hbm.1, bf16[128,4096]{1,0:T(8,128)(2,1)} %gl_hbm.1, s32[1,128]{1,0:T(1,128)} %bitcast.1, f32[7,256]{1,0:T(8,128)} %se_hbm.1, bf16[256,512]{1,0:T(8,128)(2,1)} %h_hbm.1), custom_call_target="tpu_custom_call" | custom-call | tf_op jit(solution)/shard_map/pallas_call | solution.py:486
  32.5 1.0 %copy.9 = bf16[128,4096]{1,0:T(8,128)(2,1)} copy(bf16[128,4096]{1,0:T(8,128)(2,1)S(1)} %shard_map.73) | data formatting | bytes 2097152

commit v6 on v5

--- a/solution.py
+++ b/solution.py
@@ -184,10 +184,6 @@
     lax.fori_loop(0, FIRST, short_body, 0)
 
     pl.semaphore_wait(barrier, peers)
-    pl.when(me + 1 < count)(lambda: rim_copy(me + 1).start())
-    for d in range(1, REACH + 1):
-        pl.when(me + d < count)(lambda d=d: doc_copy(d, me + d).start())
-
     def send_msg(j, _):
         send_own(msg(j))
         return 0
@@ -204,7 +200,12 @@
         block = got.at[2, pl.ds(m * each, each), pl.ds(RIM, body_rows)]
         return remote(via.at[side(i)], block, fwd_send.at[i], recv_sem.at[2, m], target)
 
-    lax.fori_loop(0, FIRST, send_msg, 0)
+    send_msg(0, 0)
+    pl.when(me + 1 < count)(lambda: rim_copy(me + 1).start())
+    for d in range(1, REACH + 1):
+        pl.when(me + d < count)(lambda d=d: doc_copy(d, me + d).start())
+
+    lax.fori_loop(1, FIRST, send_msg, 0)
     await_pieces(GROUPS - 1)
     lax.fori_loop(direct, MSGS, short_body, 0)
     for i in range(VIA):

time: 33.9 us -> 35.2 us (1.038)
  Pallas kernels: 32.5 us -> 33.8 us
    pallas_call x1, Pallas kernels: 32.5 us -> 33.8 us  [body(): pl.pallas_call(functools.partial(kernel, count), out_shape=pltpu.VMEM((ro...]
where the time goes in v6:
time: 35.2 us; the launch traced here: 34.8 us
  Pallas kernels  33.8 us (96%)
  local copies, waits for them, and re-layouts  0.97 us (3%)
    pallas_call x1, Pallas kernels, body(): pl.pallas_call(functools.partial(kernel, count), out_shape=pltpu.VMEM((ro...  33.8 us
    unnamed x1, local copies, waits for them, and re-layouts  0.97 us

profile of v6, /device:TPU:10, one launch (start us, length us, event | category | flops | bytes accessed | tf_op | source)
XLA Modules:
  0.0 34.8 jit_solution(13945965019448171241)
XLA Ops:
  0.0 33.8 %shard_map.73 = bf16[128,4096]{1,0:T(8,128)(2,1)S(1)} custom-call(bf16[128,4096]{1,0:T(8,128)(2,1)} %gs_hbm.1, bf16[128,4096]{1,0:T(8,128)(2,1)} %k_hbm.1, bf16[128,4096]{1,0:T(8,128)(2,1)} %v_hbm.1, bf16[128,4096]{1,0:T(8,128)(2,1)} %gl_hbm.1, s32[1,128]{1,0:T(1,128)} %bitcast.1, f32[7,256]{1,0:T(8,128)} %se_hbm.1, bf16[256,512]{1,0:T(8,128)(2,1)} %h_hbm.1), custom_call_target="tpu_custom_call" | custom-call | tf_op jit(solution)/shard_map/pallas_call | solution.py:487
  33.8 1.0 %copy.9 = bf16[128,4096]{1,0:T(8,128)(2,1)} copy(bf16[128,4096]{1,0:T(8,128)(2,1)S(1)} %shard_map.73) | data formatting | bytes 2097152
